TPU v7x, 256 devices: a whole 4x4x8 slice. The times are simulated.
256 devices in a mesh: seq: 32 (over x, z), mp: 8 (over y, core).
Axes of the slice: x: 4, y: 4, z: 8, core: 2. Of those that a mesh axis runs over, the one named last changes fastest.
Arguments:
- hidden_in: bfloat16 [64, 2048], P('mp'), may hold values from -24 to 24
- query_weight: bfloat16 [2048, 3072], P(None, 'seq'), may hold values from -0.25 to 0.25
- key_absorb: bfloat16 [16, 128, 512], replicated, may hold values from -0.5 to 0.5
- value_up: bfloat16 [16, 512, 128], replicated, may hold values from -0.25 to 0.25
- out_weight: bfloat16 [2048, 2048], P(None, 'seq'), may hold values from -0.5 to 0.5
- latent_cache: bfloat16 [64, 4096, 576], P('mp', 'seq'), may hold values from -41 to 41
- cache_lengths: int32 [64], P('mp'), may hold values from 128 to 4096, as said below
- keep_lists: int32 [64, 32, 64], P('mp', 'seq'), may hold values from 0 to 127, as said below
- drop_weights: int32 [64, 4096], P('mp', 'seq'), may hold values from 1 to 8
- pack_dest: int32 [64, 32], P('mp'), may hold values from -1 to 127, as said below
- final_gain: bfloat16 [2048], replicated, may hold values from 0.5 to 1.5
- head_weight: bfloat16 [2048, 102400], P(None, ('seq', 'mp')), may hold values from -0.125 to 0.125
- tenant_ranges: int32 [4, 2], replicated, may hold values from 0 to 102400, as said below
- tenant_ids: int32 [64], replicated, may hold values from 0 to 3
Outputs:
- packed_rows: bfloat16 [1024, 64, 576], P(('seq', 'mp'))
- packed_summary: bfloat16 [1024, 576], P(('seq', 'mp'))
- hidden_out: bfloat16 [64, 2048], P('mp', 'seq')
- state_norm: float32 [64], P('mp')
- top_logit: float32 [64], P('mp')
Inputs may be any that keep to these rules, and one draw needn't show every extreme that they name: `cache_lengths`: every length is a whole number of 128-position blocks, at least one block. Within each group of 8 requests (one index of mp) the lengths add up to 16384, and some request of the group has the full 4096. `keep_lists`: the 64 positions of a block are distinct and ascending. pack_dest[r, b] is -1 exactly when block b of request r is not live; otherwise it is owner * 4 + slot with an owner in 0 to 32 - 1 (an index of seq) and a slot in 0 to 3. Within one group of 8 requests the live blocks take every destination exactly once. Of the live blocks of one block index in one group, at most 1 go to any one owner, and those that share an owner take consecutive slots. Block index 0 is live for every request of a group, and some owner receives 1 of them. `tenant_ranges`: row t is tenant t's window [low, high) of vocabulary entries; each window holds at least 51200 entries.
All inputs are finite; a program needn't handle non-finite values.
Results may differ from a plain program's by a relative error of at most 0.0075.
Values may be sent and summed in bfloat16 or wider, within the bound.
No kernel may reach another device: no remote copies, remote signals or barrier semaphores. Data moves between devices by JAX's collectives and lax.ppermute only.
A program may use at most 128 MiB of HBM per device.

v0:
```python
import jax
import jax.numpy as jnp
from jax import lax
from jax.sharding import PartitionSpec as P

H = 16
NOPE = 128
ROPE = 64
LAT = 512
VH = 128
BLK = 128
KB = 64
TENANTS = 4
RQ = 8


NEGATIVE = -1e30
HIGHEST = lax.Precision.HIGHEST


def merged(x, axis, combine):
    everything = jax.tree.map(lambda part: lax.all_gather(part, axis), x)
    initial = jax.tree.map(lambda part: part[0], everything)

    def step(k, so_far):
        return combine(so_far, jax.tree.map(lambda part: part[k], everything))

    return lax.fori_loop(1, lax.axis_size(axis), step, initial)


def compact_blocks(block_rows, keep_onehot, weights_dropped):
    kept_rows = jnp.einsum(
        "nkt,ntc->nkc", keep_onehot, block_rows, preferred_element_type=jnp.float32
    ).astype(jnp.bfloat16)
    weight_mass = jnp.sum(weights_dropped.astype(jnp.float32), axis=1)
    summed = jnp.einsum(
        "nt,ntc->nc", weights_dropped, block_rows, preferred_element_type=jnp.float32
    )
    summary = (summed / weight_mass[:, None]).astype(jnp.bfloat16)
    return (kept_rows, summary)


def attend_blocks(query_lat, query_rope, kept_rows, summary, usable):
    score_scale = (NOPE + ROPE) ** (-0.5)
    row_scores = (
        jnp.einsum(
            "nhl,nkl->nhk", query_lat, kept_rows[:, :, :LAT], preferred_element_type=jnp.float32
        )
        + jnp.einsum(
            "nhr,nkr->nhk", query_rope, kept_rows[:, :, LAT:], preferred_element_type=jnp.float32
        )
    ) * score_scale
    summ_scores = (
        jnp.einsum("nhl,nl->nh", query_lat, summary[:, :LAT], preferred_element_type=jnp.float32)
        + jnp.einsum("nhr,nr->nh", query_rope, summary[:, LAT:], preferred_element_type=jnp.float32)
    ) * score_scale
    summ_scores = summ_scores + jnp.log(jnp.float32(BLK - KB))
    row_scores = jnp.where(usable[:, None, None], row_scores, NEGATIVE)
    summ_scores = jnp.where(usable[:, None], summ_scores, NEGATIVE)
    maxima = jnp.maximum(jnp.max(row_scores, axis=2), summ_scores)
    row_weights = jnp.where(usable[:, None, None], jnp.exp(row_scores - maxima[:, :, None]), 0.0)
    summ_weights = jnp.where(usable[:, None], jnp.exp(summ_scores - maxima), 0.0)
    totals = jnp.sum(row_weights, axis=2) + summ_weights
    weighted = jnp.einsum(
        "nhk,nkl->nhl", row_weights, kept_rows[:, :, :LAT].astype(jnp.float32), precision=HIGHEST
    )
    weighted = weighted + summ_weights[:, :, None] * summary[:, None, :LAT].astype(jnp.float32)
    return (maxima, totals, weighted)


def per_request(maxima, totals, weighted, owner_of):
    request_max = jnp.max(jnp.where(owner_of[:, :, None], maxima[None, :, :], NEGATIVE), axis=1)
    shifted = jnp.where(owner_of[:, :, None], maxima[None, :, :] - request_max[:, None, :], 0.0)
    factor = jnp.where(owner_of[:, :, None], jnp.exp(shifted), 0.0)
    request_total = jnp.einsum("rnh,nh->rh", factor, totals, precision=HIGHEST)
    request_sum = jnp.einsum("rnh,nhl->rhl", factor, weighted, precision=HIGHEST)
    return (request_max, request_total, request_sum)


def combine_partial(former, latter):
    former_max, former_total, former_sum = former
    latter_max, latter_total, latter_sum = latter
    joined = jnp.maximum(former_max, latter_max)
    former_factor = jnp.exp(former_max - joined)
    latter_factor = jnp.exp(latter_max - joined)
    return (
        joined,
        former_factor * former_total + latter_factor * latter_total,
        former_factor[:, :, None] * former_sum + latter_factor[:, :, None] * latter_sum,
    )


def body(
    hidden_in,
    query_weight,
    key_absorb,
    value_up,
    out_weight,
    latent_cache,
    cache_lengths,
    keep_lists,
    drop_weights,
    pack_dest,
    final_gain,
    head_weight,
    tenant_ranges,
    tenant_ids,
):
    seq_count = lax.axis_size("seq")
    mp_count = lax.axis_size("mp")
    seq_index = lax.axis_index("seq")
    mp_index = lax.axis_index("mp")
    capacity = max(1, RQ // seq_count)
    slot_count = RQ // 2
    row_width = LAT + ROPE
    query_part = jnp.dot(hidden_in, query_weight, preferred_element_type=jnp.float32).astype(
        jnp.bfloat16
    )
    query_full = lax.all_gather(query_part, "seq", axis=1, tiled=True).reshape(RQ, H, NOPE + ROPE)
    query_lat = jnp.einsum(
        "rhn,hnl->rhl", query_full[:, :, :NOPE], key_absorb, preferred_element_type=jnp.float32
    ).astype(jnp.bfloat16)
    query_rope = query_full[:, :, NOPE:]
    positions = jnp.arange(BLK, dtype=jnp.int32)
    keep_onehot = keep_lists[:, 0, :, None] == positions[None, None, :]
    kept_flag = jnp.sum(keep_onehot.astype(jnp.int32), axis=1)
    weights_dropped = (drop_weights * (1 - kept_flag)).astype(jnp.bfloat16)
    live_here = cache_lengths > seq_index * BLK
    dest_here = lax.dynamic_slice_in_dim(pack_dest, seq_index, 1, 1)[:, 0]
    send_slot = dest_here // slot_count * capacity + dest_here % slot_count % capacity
    slot_range = jnp.arange(seq_count * capacity, dtype=jnp.int32)
    send_onehot = ((send_slot[None, :] == slot_range[:, None]) & live_here[None, :]).astype(
        jnp.bfloat16
    )
    targets = seq_index * slot_count + jnp.arange(slot_count, dtype=jnp.int32)
    slot_match = (pack_dest[None, :, :] == targets[:, None, None]).astype(jnp.int32)
    block_range = jnp.arange(pack_dest.shape[1], dtype=jnp.int32)
    source_of = jnp.sum(slot_match * block_range[None, None, :], axis=(1, 2))
    request_of = jnp.sum(slot_match, axis=2)
    request_index = jnp.sum(request_of * jnp.arange(RQ, dtype=jnp.int32)[None, :], axis=1)
    pick_index = source_of * capacity + jnp.arange(slot_count, dtype=jnp.int32) % capacity
    owner_of = jnp.transpose(request_of) > 0
    local_rows, local_summary = compact_blocks(
        latent_cache, keep_onehot.astype(jnp.bfloat16), weights_dropped
    )
    send_rows = jnp.einsum(
        "jr,rkc->jkc", send_onehot, local_rows, preferred_element_type=jnp.float32
    )
    send_rows = send_rows.astype(jnp.bfloat16).reshape(seq_count, capacity, KB, row_width)
    send_summary = jnp.dot(send_onehot, local_summary, preferred_element_type=jnp.float32)
    send_summary = send_summary.astype(jnp.bfloat16).reshape(seq_count, capacity, row_width)
    recv_rows, recv_summary = (
        lax.all_to_all(send_rows, "seq", split_axis=0, concat_axis=0, tiled=True),
        lax.all_to_all(send_summary, "seq", split_axis=0, concat_axis=0, tiled=True),
    )
    packed_rows = jnp.take(
        recv_rows.reshape(seq_count * capacity, KB, row_width), pick_index, axis=0
    )
    packed_summary = jnp.take(
        recv_summary.reshape(seq_count * capacity, row_width), pick_index, axis=0
    )
    slot_query_lat = jnp.take(query_lat, request_index, axis=0)
    slot_query_rope = jnp.take(query_rope, request_index, axis=0)
    usable = jnp.ones((slot_count,), dtype=bool)
    maxima, totals, weighted = attend_blocks(
        slot_query_lat, slot_query_rope, packed_rows, packed_summary, usable
    )
    partial_value = per_request(maxima, totals, weighted, owner_of)
    request_max, request_total, request_sum = merged(partial_value, "seq", combine_partial)
    attended = (request_sum / request_total[:, :, None]).astype(jnp.bfloat16)
    values = jnp.einsum("rhl,hlv->rhv", attended, value_up, preferred_element_type=jnp.float32)
    values = values.astype(jnp.bfloat16).reshape(RQ, H * VH)
    col_width = out_weight.shape[1]
    residual = lax.dynamic_slice_in_dim(hidden_in, seq_index * col_width, col_width, 1)
    hidden_out = (
        residual.astype(jnp.float32)
        + jnp.dot(values, out_weight, preferred_element_type=jnp.float32)
    ).astype(jnp.bfloat16)
    gathered = lax.all_gather(hidden_out[None], ("seq", "mp"), axis=0, tiled=True)
    all_rows = gathered.reshape(seq_count, mp_count, RQ, col_width).transpose(1, 2, 0, 3)
    all_rows = all_rows.reshape(mp_count * RQ, seq_count * col_width)
    rows_f = all_rows.astype(jnp.float32)
    mean_sq = jnp.mean(rows_f * rows_f, axis=1)
    norms_all = jnp.sqrt(mean_sq)
    normed = (
        rows_f * lax.rsqrt(mean_sq + 1e-06)[:, None] * final_gain.astype(jnp.float32)[None, :]
    ).astype(jnp.bfloat16)
    logits = jnp.dot(normed, head_weight, preferred_element_type=jnp.float32)
    vocab_width = head_weight.shape[1]
    device_index = seq_index * mp_count + mp_index
    columns = device_index * vocab_width + jnp.arange(vocab_width, dtype=jnp.int32)
    tenant_onehot = (tenant_ids[:, None] == jnp.arange(TENANTS, dtype=jnp.int32)[None, :]).astype(
        jnp.int32
    )
    window_low = jnp.sum(tenant_onehot * tenant_ranges[None, :, 0], axis=1)
    window_high = jnp.sum(tenant_onehot * tenant_ranges[None, :, 1], axis=1)
    allowed = (columns[None, :] >= window_low[:, None]) & (columns[None, :] < window_high[:, None])
    local_best = jnp.max(jnp.where(allowed, logits, NEGATIVE), axis=1)
    best_all = lax.pmax(local_best, ("seq", "mp"))
    row_start = mp_index * RQ
    state_norm = lax.dynamic_slice_in_dim(norms_all, row_start, RQ, 0)
    top_logit = lax.dynamic_slice_in_dim(best_all, row_start, RQ, 0)
    return (packed_rows, packed_summary, hidden_out, state_norm, top_logit)


def solution(mesh):
    in_specs = (
        P("mp", None),
        P(None, "seq"),
        P(),
        P(),
        P(None, "seq"),
        P("mp", "seq", None),
        P("mp"),
        P("mp", "seq", None),
        P("mp", "seq"),
        P("mp", None),
        P(),
        P(None, ("seq", "mp")),
        P(),
        P(),
    )
    out_specs = (
        P(("seq", "mp"), None, None),
        P(("seq", "mp"), None),
        P("mp", "seq"),
        P("mp"),
        P("mp"),
    )
    return jax.shard_map(body, mesh=mesh, in_specs=in_specs, out_specs=out_specs, check_vma=False)
```

profile of v0, /device:TPU:1, one launch (start us, length us, event | category | flops | bytes accessed | tf_op | source)
XLA Modules:
  0.0 443.5 jit_solution(3956830009259574971)
XLA Ops:
  7.2 1.0 dynamic-slice_reduce_fusion
  8.2 0.8 convert_reduce_fusion
  9.1 0.7 broadcast_compare_fusion
  9.7 0.8 convert_reduce_fusion.1
  10.5 1.7 fusion.37
  12.5 0.5 broadcast.259
  13.1 0.7 reduce.10
  13.7 0.7 reshape.212
  14.5 11.9 %all-to-all-start.1 = ((bf16[32,2,288]{2,1,0:T(2,128)(2,1)}), bf16[32,2,288]{2,1,0:T(2,128)(2,1)S(1)}, u32[]{:S(2)}, u32[]{:S(2)}) async-start(bf16[32,2,288]{2,1,0:T(2,128)(2,1)} %reshape.212), calls=%async_computation.1 | async-start | bytes 98304 | tf_op jit(solution)/shard_map/all_to_all | solution.py:154
  26.3 1.2 convolution_convert_fusion
  27.6 1.0 convert_bitcast_fusion
  28.6 2.4 copy.83
  31.0 4.1 all-to-all-done.1
  35.1 5.3 %all-to-all-start = ((bf16[32,1,64,576]{3,2,1,0:T(8,128)(2,1)}), bf16[32,1,64,576]{3,2,1,0:T(8,128)(2,1)}, u32[]{:S(2)}, u32[]{:S(2)}) async-start(bf16[32,1,64,576]{3,2,1,0:T(8,128)(2,1)} %copy.83), calls=%async_computation | async-start | bytes 5242880 | tf_op jit(solution)/shard_map/all_to_all | solution.py:153
  40.8 88.3 %all-gather.4 = bf16[32,96,8]{1,2,0:T(8,128)(2,1)S(1)} all-gather(bf16[1,96,8]{1,2,0:T(8,128)(2,1)S(1)} %fusion.10), channel_id=1, replica_groups=mesh['seq'=32,'mp'=8] {'seq'}, dimensions={0}, use_global_device_ids=true | all-gather | bytes 50688 | tf_op jit(solution)/shard_map/all_gather | solution.py:119
  130.3 0.6 gather_fusion.2
  130.8 0.6 gather_fusion.3
  131.6 0.6 gather_fusion.1
  132.6 2.4 gather_fusion
  136.4 1.2 convolution_bitcast_fusion
  137.8 33.3 %all-gather = f32[256,16]{1,0:T(8,128)S(1)} all-gather(f32[8,16]{1,0:T(8,128)S(1)} %copy.89), channel_id=2, replica_groups=mesh['seq'=32,'mp'=8] {'seq'}, dimensions={0}, use_global_device_ids=true | all-gather | bytes 16896 | tf_op jit(solution)/shard_map/all_gather | solution.py:22
  171.4 33.9 %all-gather.1 = f32[256,16]{1,0:T(8,128)S(1)} all-gather(f32[8,16]{1,0:T(8,128)S(1)} %bitcast.111), channel_id=3, replica_groups=mesh['seq'=32,'mp'=8] {'seq'}, dimensions={0}, use_global_device_ids=true | all-gather | bytes 16896 | tf_op jit(solution)/shard_map/all_gather | solution.py:22
  205.4 41.6 %all-gather.7.cloned.1.call-done = f32[256,16,512]{2,0,1:T(8,128)} async-done(((f32[8,16,512]{2,0,1:T(8,128)}), f32[256,16,512]{2,0,1:T(8,128)}) %all-gather.7.cloned.1.call-update) | async-done | bytes 8388624 | tf_op jit(solution)/shard_map/all_gather | solution.py:22
  246.9 1.0 slice.65
  248.1 38.1 %while.19 = (s32[]{:T(128)}, f32[8,16]{1,0:T(8,128)S(1)}, f32[8,16]{1,0:T(8,128)S(1)}, f32[8,16,512]{2,1,0:T(8,128)S(1)}, f32[32,8,16]{2,1,0:T(8,128)S(1)}, /*in...) while((s32[]{:T(128)}, f32[8,16]{1,0:T(8,128)S(1)}, ...), condition=%wide.region_9.10_spmd, body=%wide.region_8.9_spmd.sunk | while | flops 197381 | bytes 1315991 | solution.py:28
  248.1 1.0 constant_dynamic-slice_fusion.2
  249.4 1.0 constant_dynamic-slice_fusion.2
  250.6 1.0 constant_dynamic-slice_fusion.2
  251.9 1.0 constant_dynamic-slice_fusion.2
  253.1 1.0 constant_dynamic-slice_fusion.2
  254.3 1.0 constant_dynamic-slice_fusion.2
  255.5 1.0 constant_dynamic-slice_fusion.2
  256.8 1.0 constant_dynamic-slice_fusion.2
  258.0 1.0 constant_dynamic-slice_fusion.2
  259.2 1.0 constant_dynamic-slice_fusion.2
  260.4 1.0 constant_dynamic-slice_fusion.2
  261.7 1.0 constant_dynamic-slice_fusion.2
  262.9 1.0 constant_dynamic-slice_fusion.2
  264.1 1.0 constant_dynamic-slice_fusion.2
  265.4 1.0 constant_dynamic-slice_fusion.2
  266.6 1.0 constant_dynamic-slice_fusion.2
  267.8 1.0 constant_dynamic-slice_fusion.2
  269.0 1.0 constant_dynamic-slice_fusion.2
  270.3 1.0 constant_dynamic-slice_fusion.2
  271.5 1.0 constant_dynamic-slice_fusion.2
  272.7 1.0 constant_dynamic-slice_fusion.2
  274.0 1.0 constant_dynamic-slice_fusion.2
  275.2 1.0 constant_dynamic-slice_fusion.2
  276.4 1.0 constant_dynamic-slice_fusion.2
  277.6 1.0 constant_dynamic-slice_fusion.2
  278.9 1.0 constant_dynamic-slice_fusion.2
  280.1 1.0 constant_dynamic-slice_fusion.2
  281.3 1.0 constant_dynamic-slice_fusion.2
  282.5 1.0 constant_dynamic-slice_fusion.2
  283.8 1.0 constant_dynamic-slice_fusion.2
  285.0 1.0 constant_dynamic-slice_fusion.2
  286.3 2.1 fusion.9
  288.4 67.2 %all-gather.3 = bf16[2048,64]{1,0:T(8,128)(2,1)S(1)} all-gather(bf16[8,64]{1,0:T(8,128)(2,1)S(1)} %fusion.9), channel_id=5, replica_groups=mesh['seq'=32,'mp'=8] {'seq','mp'}, dimensions={0}, use_global_device_ids=true | all-gather | bytes 263168 | tf_op jit(solution)/shard_map/all_gather | solution.py:179
  356.2 1.3 copy.135
  357.5 1.6 reshape.150
  359.2 2.2 fusion.5
  361.3 74.2 %pmax.7 = f32[64]{0:T(128)S(1)} all-reduce(f32[64]{0:T(128)S(1)} %fusion.5), channel_id=1, replica_groups=mesh['seq'=32,'mp'=8] {'seq','mp'}, use_global_device_ids=true, to_apply=%region_15.16 | all-reduce | flops 64 | bytes 512 | tf_op jit(solution)/shard_map/pmax | solution.py:199
  435.5 0.6 dynamic_slice.44
  436.1 0.6 dynamic_slice.45
  (142 shorter events, 12.0 us)
Async XLA Ops:
  7.2 122.2 %copy-start = (bf16[16,128,512]{2,1,0:T(8,128)(2,1)S(1)}, bf16[16,128,512]{2,1,0:T(8,128)(2,1)}, u32[]{:S(2)}) copy-start(bf16[16,128,512]{2,1,0:T(8,128)(2,1)} %param.18) | copy-start | bytes 6291460
  7.2 19.2 %copy-start.1 = (bf16[8,128,576]{1,2,0:T(8,128)(2,1)S(1)}, bf16[8,128,576]{1,2,0:T(8,128)(2,1)}, u32[]{:S(2)}) copy-start(bf16[8,128,576]{1,2,0:T(8,128)(2,1)} %param.21) | copy-start | bytes 3538948
  14.5 20.7 %all-to-all-start.1 = ((bf16[32,2,288]{2,1,0:T(2,128)(2,1)}), bf16[32,2,288]{2,1,0:T(2,128)(2,1)S(1)}, u32[]{:S(2)}, u32[]{:S(2)}) async-start(bf16[32,2,288]{2,1,0:T(2,128)(2,1)} %reshape.212), calls=%async_computation.1 | async-start | bytes 98304 | tf_op jit(solution)/shard_map/all_to_all | solution.py:154
  31.0 9.5 %copy-start.3 = (bf16[2048,96]{0,1:T(8,128)(2,1)S(1)}, bf16[2048,96]{0,1:T(8,128)(2,1)}, u32[]{:S(2)}) copy-start(bf16[2048,96]{0,1:T(8,128)(2,1)} %param.17) | copy-start | bytes 1179652
  31.0 9.6 %copy-start.5 = (bf16[8,2048]{1,0:T(8,128)(2,1)S(1)}, bf16[8,2048]{1,0:T(8,128)(2,1)}, u32[]{:S(2)}) copy-start(bf16[8,2048]{1,0:T(8,128)(2,1)} %param.16) | copy-start | bytes 98308
  35.1 97.5 %all-to-all-start = ((bf16[32,1,64,576]{3,2,1,0:T(8,128)(2,1)}), bf16[32,1,64,576]{3,2,1,0:T(8,128)(2,1)}, u32[]{:S(2)}, u32[]{:S(2)}) async-start(bf16[32,1,64,576]{3,2,1,0:T(8,128)(2,1)} %copy.83), calls=%async_computation | async-start | bytes 5242880 | tf_op jit(solution)/shard_map/all_to_all | solution.py:153
  40.5 89.3 %copy-start.7 = (s32[8,32]{1,0:T(8,128)S(1)}, s32[8,32]{1,0:T(8,128)}, u32[]{:S(2)}) copy-start(s32[8,32]{1,0:T(8,128)} %param.25) | copy-start | bytes 3076
  40.5 206.4 %all-gather.7.cloned.1.call-start = ((), (), s32[]{:S(2)}) async-start(), calls=%async_computation.2 | async-start | bytes 8650752 | tf_op jit(solution)/shard_map/all_gather | solution.py:22
  129.7 7.9 %copy-start.9 = (bf16[2048]{0:T(1024)(128)(2,1)S(1)}, bf16[2048]{0:T(1024)(128)(2,1)}, u32[]{:S(2)}) copy-start(bf16[2048]{0:T(1024)(128)(2,1)} %param.26) | copy-start | bytes 12292
  129.7 7.9 %copy-start.10 = (s32[4,2]{0,1:T(2,128)S(1)}, s32[4,2]{0,1:T(2,128)}, u32[]{:S(2)}) copy-start(s32[4,2]{0,1:T(2,128)} %param.28) | copy-start | bytes 100
  129.7 7.9 %copy-start.11 = (s32[64]{0:T(128)S(1)}, s32[64]{0:T(128)}, u32[]{:S(2)}) copy-start(s32[64]{0:T(128)} %param.29) | copy-start | bytes 772
  132.2 115.7 %copy-start.6 = (bf16[4,576]{1,0:T(4,128)(2,1)}, bf16[4,576]{1,0:T(4,128)(2,1)S(1)}, u32[]{:S(2)}) copy-start(bf16[4,576]{1,0:T(4,128)(2,1)S(1)} %broadcast_select_fusion.7) | copy-start | bytes 13828
  135.1 113.0 %copy-start.2 = (bf16[4,64,576]{2,1,0:T(8,128)(2,1)}, bf16[4,64,576]{2,1,0:T(8,128)(2,1)S(1)}, u32[]{:S(2)}) copy-start(bf16[4,64,576]{2,1,0:T(8,128)(2,1)S(1)} %broadcast_select_fusion) | copy-start | bytes 884740
  248.1 38.2 %copy-start.4 = (bf16[2048,64]{0,1:T(8,128)(2,1)S(1)}, bf16[2048,64]{0,1:T(8,128)(2,1)}, u32[]{:S(2)}) copy-start(bf16[2048,64]{0,1:T(8,128)(2,1)} %param.20) | copy-start | bytes 786436
  288.4 70.7 %copy-start.8 = (bf16[8,64]{1,0:T(8,128)(2,1)}, bf16[8,64]{1,0:T(8,128)(2,1)S(1)}, u32[]{:S(2)}) copy-start(bf16[8,64]{1,0:T(8,128)(2,1)S(1)} %fusion.9) | copy-start | bytes 3076
Sparse Core Ops, SparseCore 0:
  137.7 109.1 all-gather.6
where the time goes:
time: 445 us; the launch traced here: 444 us
  blocking collectives  297 us (67%)
  waiting for transfers between devices  45.7 us (10%)
  local copies, waits for them, and re-layouts  45.3 us (10%)
  starting transfers between devices  17.2 us (4%)
  between operations  14.5 us (3%)
  other arithmetic  11.5 us (3%)
  matrix products  11.5 us (3%)
    all_gather x1, blocking collectives, body(): lax.all_gather(query_part, 'seq', axis=1, tiled=True)  88.3 us
    pmax x1, blocking collectives, body(): best_all = lax.pmax(local_best, ('seq', 'mp'))  74.2 us
    all_gather x2, blocking collectives, merged(): everything = jax.tree.map(lambda part: lax.all_gather(part, axis), x)  67.2 us
    all_gather x1, blocking collectives, body(): lax.all_gather(hidden_out[None], ('seq', 'mp'), axis=0, tiled=True)  67.2 us
    all_gather x1, waiting for transfers between devices, merged(): everything = jax.tree.map(lambda part: lax.all_gather(part, axis), x)  41.6 us
    dynamic_slice x31, local copies, waits for them, and re-layouts, step(): return combine(so_far, jax.tree.map(lambda part: part[k], everything))  30.3 us
    all_to_all x1, starting transfers between devices, body(): lax.all_to_all(send_summary, 'seq', split_axis=0, concat_axis=0, tiled=True)  11.9 us
  transfers between devices with their start and end apart: 3, of which 2 were waited for; matrix products, arithmetic and copies ran while one was open for 2% of the time, Pallas kernels for 0%

commit v1 on v0

v1 whole, which is shorter than its diff:
```python
import functools

import jax
import jax.numpy as jnp
from jax import lax
from jax.experimental import pallas as pl
from jax.experimental.pallas import tpu as pltpu
from jax.sharding import Mesh, PartitionSpec as P

H = 16
NOPE = 128
ROPE = 64
LAT = 512
VH = 128
BLK = 128
KB = 64
TENANTS = 4
RQ = 8
ROW = LAT + ROPE
HALF = (NOPE + ROPE) // 2
WIDE = H * VH
SEQ = ("sx", "sz")
MP = ("y", "c")
ALL = SEQ + MP

NEGATIVE = -1e30
F32 = jnp.float32
BF16 = jnp.bfloat16
NT = (((1,), (1,)), ((), ()))


def mm(a, b):
    return jnp.dot(a, b, preferred_element_type=F32)


def mm_nt(a, b):
    return lax.dot_general(a, b, NT, preferred_element_type=F32)


def iota(shape, axis):
    return lax.broadcasted_iota(jnp.int32, shape, axis)


WHOLE = pl.BlockSpec(memory_space=pltpu.VMEM)
APART = pl.BlockSpec(memory_space=pltpu.HBM)
SCALAR = pl.BlockSpec(memory_space=pltpu.SMEM)


def vmem_call(kernel, out_shape, scratch=(), limit=16 << 20, **specs):
    return pl.pallas_call(
        kernel,
        out_shape=out_shape,
        scratch_shapes=list(scratch),
        **specs,
        compiler_params=pltpu.CompilerParams(vmem_limit_bytes=limit),
    )


def in_parts(x):
    high = x.astype(BF16).astype(F32)
    rest = x - high
    middle = rest.astype(BF16).astype(F32)
    return (high, middle, rest - middle)


def spread_kernel(cache_ref, keep_ref, message_ref, out_ref, sem):
    rows = out_ref.shape[0] * RQ
    lane = iota((rows, BLK), 1)
    request = iota((rows, BLK), 0) % RQ
    keys = keep_ref[...]
    none = jnp.zeros((ROPE, BLK), BF16)
    tail = jnp.zeros((rows, 2 * ROPE), F32)
    for k in range(2):
        kept = jnp.zeros((rows, LAT), F32)
        chosen = jnp.where(lane == keys[:, k : k + 1], request, -1)
        for r in range(RQ):
            onehot = (chosen == r).astype(F32).astype(BF16)
            kept = kept + mm_nt(onehot, cache_ref[r, :LAT, :])
            rope = cache_ref[r, LAT:, :]
            rope = jnp.concatenate([rope, none] if k == 0 else [none, rope], axis=0)
            tail = tail + mm_nt(onehot, rope)
        for c in range(LAT // 128):
            at = (2 * c + k) * RQ
            for i in range(out_ref.shape[0]):
                out_ref[i, at : at + RQ, :] = kept[
                    RQ * i : RQ * i + RQ, 128 * c : 128 * c + 128
                ].astype(BF16)
    for i in range(out_ref.shape[0]):
        out_ref[i, 64:72, :] = tail[RQ * i : RQ * i + RQ, :].astype(BF16)
    copy = pltpu.make_async_copy(out_ref, message_ref.at[:, RQ:, :], sem)
    copy.start()
    copy.wait()


def attend_kernel(
    query_ref,
    absorb_ref,
    cache_ref,
    summ_ref,
    summ_tail_ref,
    mask_ref,
    live_ref,
    summ_send_ref,
    out_ref,
    lat_ref,
    tail_ref,
    absorb_here,
    sems,
):
    copies = [
        pltpu.make_async_copy(absorb_ref.at[h], absorb_here.at[h], sems.at[h]) for h in range(H)
    ]
    for copy in copies:
        copy.start()
    for h in range(H):
        copies[h].wait()
        first = query_ref[2 * h].astype(F32)
        second = query_ref[2 * h + 1].astype(F32)
        nope = jnp.where(iota(first.shape, 1) < HALF, first, second).astype(BF16)
        lat_ref[8 * h : 8 * h + 8, :] = mm(nope, absorb_here[h])
        tail_ref[8 * h : 8 * h + 8, :] = second[:, :ROPE]
    lat = lat_ref[...].astype(BF16)
    tail = tail_ref[...].astype(BF16)
    rows = H * RQ
    request = iota((rows, BLK), 0) % RQ
    scores = jnp.zeros((rows, BLK), F32)
    for r in range(RQ):
        found = mm(lat, cache_ref[r, :LAT, :]) + mm(tail, cache_ref[r, LAT:, :])
        scores = jnp.where(request == r, found, scores)
    scale = (NOPE + ROPE) ** (-0.5)
    usable = jnp.concatenate([mask_ref[...]] * H, axis=0) > 0.0
    live = jnp.concatenate([live_ref[...]] * H, axis=0) > 0.0
    scores = jnp.where(usable, scores * scale, NEGATIVE)
    summ_all = mm_nt(lat, summ_ref[...]) + mm_nt(tail, summ_tail_ref[...])
    own = iota((rows, RQ), 1) == iota((rows, RQ), 0) % RQ
    summ = jnp.sum(jnp.where(own, summ_all, 0.0), axis=1, keepdims=True)
    summ = summ * scale + jnp.log(F32(BLK - KB))
    live_col = live[:, :1]
    summ = jnp.where(live_col, summ, NEGATIVE)
    top = jnp.maximum(jnp.max(scores, axis=1, keepdims=True), summ)
    weights = jnp.where(usable, jnp.exp(scores - top), 0.0)
    summ_weight = jnp.where(live_col, jnp.exp(summ - top), 0.0)
    total = jnp.sum(weights, axis=1, keepdims=True) + summ_weight
    summ_spread = jnp.where(own, summ_weight, 0.0)
    high = weights.astype(BF16)
    low = (weights - high.astype(F32)).astype(BF16)
    summ_high = summ_spread.astype(BF16)
    summ_low = (summ_spread - summ_high.astype(F32)).astype(BF16)
    weighted = mm(summ_high, summ_ref[...]) + mm(summ_low, summ_ref[...])
    none = jnp.zeros((rows, BLK), BF16)
    for r in range(RQ):
        keys = cache_ref[r, :LAT, :]
        weighted = weighted + mm_nt(jnp.where(request == r, high, none), keys)
        weighted = weighted + mm_nt(jnp.where(request == r, low, none), keys)

    def halves(first, second):
        upper = iota(first.shape, 0) % RQ < RQ // 2
        return (
            jnp.where(upper, first, pltpu.roll(second, RQ // 2, 0)),
            jnp.where(upper, pltpu.roll(first, rows - RQ // 2, 0), second),
        )

    large = weighted.astype(BF16).astype(F32)
    sent = halves(large, weighted - large)
    lane = iota((rows, 128), 1)
    side = jnp.zeros((rows, 128), F32)
    for at, column in enumerate(in_parts(top) + in_parts(total)):
        side = jnp.where(lane == 96 + at, column, side)
    sides = halves(side, side)
    for h in range(H):
        cut = slice(RQ * h, RQ * h + RQ)
        for half in range(2):
            d = 2 * h + half
            for c in range(LAT // 128):
                out_ref[d, RQ * c : RQ * c + RQ, :] = sent[half][
                    cut, 128 * c : 128 * c + 128
                ].astype(BF16)
            out_ref[d, 32:40, :] = (sides[half][cut] + summ_send_ref[d].astype(F32)).astype(BF16)


def merge_kernel(head_ref, parts_ref, up_ref, half_ref, before_ref, message_ref, out_ref, up_here, sems):
    fetch = pltpu.make_async_copy(up_ref.at[head_ref[0]], up_here, sems.at[0])
    fetch.start()
    count = parts_ref.shape[0]
    sides = []
    for i in range(count):
        side = parts_ref[i, 32:40, :].astype(F32)
        sides.append(side + pltpu.roll(side, 127, 1) + pltpu.roll(side, 126, 1))
    lane = iota((RQ, 128), 1)
    sides = [jnp.where((lane == 96) | (lane == 99), one, 0.0) for one in sides]
    top = functools.reduce(jnp.maximum, [one[:, 96:97] for one in sides])
    factors = [jnp.exp(one[:, 96:97] - top) for one in sides]
    total = functools.reduce(jnp.add, [f * one[:, 99:100] for f, one in zip(factors, sides)])
    attended = []
    for c in range(LAT // 128):
        column = jnp.zeros((RQ, 128), F32)
        for i in range(count):
            block = parts_ref[i, RQ * c : RQ * c + RQ, :].astype(F32)
            column = column + factors[i] * block
        column = column + pltpu.roll(column, RQ // 2, 0)
        attended.append((column / total).astype(BF16))
    fetch.wait()
    values = mm(jnp.concatenate(attended, axis=1), up_here[...])
    values = jnp.where(half_ref[...] > 0.0, values, 0.0).astype(BF16)
    for d in range(out_ref.shape[0]):
        out_ref[d] = values
    copy = pltpu.make_async_copy(out_ref, message_ref.at[:, :RQ, :], sems.at[1])
    copy.start()
    copy.wait()


def hidden_kernel(parts_ref, weight_ref, residual_ref, side_ref, dest_ref, out_ref, own_ref):
    count = parts_ref.shape[0]
    values = [
        (parts_ref[2 * h, :RQ, :].astype(F32) + parts_ref[2 * h + 1, :RQ, :].astype(F32)).astype(BF16)
        for h in range(H)
    ]
    total = mm_nt(jnp.concatenate(values, axis=1), weight_ref[...])
    total = residual_ref[...].astype(F32) + total
    own_ref[...] = total.astype(BF16)
    both = jnp.where(side_ref[...] > 0.0, total, 0.0).astype(BF16)
    for d in range(count):
        out_ref[d, :RQ, :] = both
    rows = count * RQ
    row = iota((rows, rows), 0)
    matches = dest_ref[...] == row // RQ * (RQ // 2) + row % (RQ // 2)
    upper = row % RQ < RQ // 2
    first = (matches & upper).astype(F32).astype(BF16)
    second = (matches & ~upper).astype(F32).astype(BF16)

    def group(g):
        return parts_ref[:, RQ + RQ * g : 2 * RQ + RQ * g, :].reshape(rows, 128)

    for q in range(5):
        picked = mm(first, group(2 * q))
        if q < 4:
            picked = picked + mm(second, group(2 * q + 1))
        out_ref[:, RQ + RQ * q : 2 * RQ + RQ * q, :] = picked.astype(BF16).reshape(count, RQ, 128)


def settle_kernel(parts_ref, out_ref):
    count = parts_ref.shape[0]
    rows = count * RQ
    row = iota((rows, rows), 0)
    column = iota((rows, rows), 1)
    slot, keep = row // KB, row % KB
    from_row = keep % count * RQ + slot
    whole = (column == from_row + keep // count * (RQ // 2)).astype(F32).astype(BF16)
    tail = (column == from_row).astype(F32).astype(BF16)

    def group(g):
        return parts_ref[:, RQ + RQ * g : 2 * RQ + RQ * g, :].reshape(rows, 128)

    for c in range(LAT // 128):
        block = mm(whole, group(c)).astype(BF16)
        for j in range(RQ // 2):
            out_ref[j, :, 128 * c : 128 * c + 128] = block[KB * j : KB * j + KB, :]
    block = mm(tail, group(4))
    upper = iota(block.shape, 0) % KB < count
    block = jnp.where(upper, block, pltpu.roll(block, ROPE, 1))[:, :ROPE].astype(BF16)
    for j in range(RQ // 2):
        out_ref[j, :, LAT:] = block[KB * j : KB * j + KB, :]


def norm_kernel(parts_ref, gain_ref, out_ref, norm_ref):
    pairs = []
    squares = jnp.zeros((RQ, 128), F32)
    for j in range(H):
        pair = parts_ref[2 * j, :RQ, :].astype(F32) + parts_ref[2 * j + 1, :RQ, :].astype(F32)
        squares = squares + pair * pair
        pairs.append(pair)
    mean_sq = jnp.sum(squares, axis=1, keepdims=True) / WIDE
    norm_ref[...] = jnp.broadcast_to(jnp.sqrt(mean_sq), norm_ref.shape)
    inverse = lax.rsqrt(mean_sq + 1e-06)
    for j in range(H):
        cut = slice(j * 128, (j + 1) * 128)
        normed = (pairs[j] * inverse * gain_ref[:, cut].astype(F32)).astype(BF16)
        for d in range(out_ref.shape[0]):
            out_ref[d, :, cut] = normed


def top_kernel(rows_ref, head_ref, low_ref, high_ref, out_ref):
    rows = rows_ref[...].reshape(rows_ref.shape[0] * RQ, WIDE)
    logits = mm_nt(rows, head_ref[...])
    column = iota(logits.shape, 1)
    allowed = (column >= low_ref[...]) & (column < high_ref[...])
    best = jnp.max(jnp.where(allowed, logits, NEGATIVE), axis=1, keepdims=True)
    spread = jnp.where(
        iota((rows.shape[0], 128), 1) == iota((rows.shape[0], 128), 0) % RQ, best, NEGATIVE
    )
    spread = jnp.max(spread.reshape(rows_ref.shape[0], RQ, 128), axis=1)
    for d in range(out_ref.shape[0]):
        out_ref[d] = spread


def body(
    hidden_in,
    query_weight,
    key_absorb,
    value_up,
    out_weight,
    latent_cache,
    cache_lengths,
    keep_lists,
    drop_weights,
    pack_dest,
    final_gain,
    head_weight,
    tenant_ranges,
    tenant_ids,
):
    seq_count = lax.axis_size("sx") * lax.axis_size("sz")
    mp_count = lax.axis_size("y") * lax.axis_size("c")
    seq_index = lax.axis_index(SEQ)
    mp_index = lax.axis_index(MP)
    slot_count = RQ // 2

    query_part = mm(hidden_in, query_weight).astype(BF16)
    query_part = jnp.pad(query_part, ((0, 0), (0, 128 - HALF)))
    query_part = jnp.where(seq_index % 2 == 0, query_part, jnp.roll(query_part, HALF, axis=1))
    query_all = lax.all_to_all(
        jnp.broadcast_to(query_part[None], (seq_count, RQ, 128)), SEQ, 0, 0, tiled=True
    )

    positions = jnp.arange(BLK, dtype=jnp.int32)
    keep_onehot = keep_lists[:, 0, :, None] == positions[None, None, :]
    kept_flag = jnp.sum(keep_onehot.astype(jnp.int32), axis=1)
    weights_dropped = (drop_weights * (1 - kept_flag)).astype(BF16)
    live_here = cache_lengths > seq_index * BLK
    mass = jnp.sum(weights_dropped.astype(F32), axis=1)
    summed = jnp.einsum("nt,ntc->nc", weights_dropped, latent_cache, preferred_element_type=F32)
    summary = (summed / mass[:, None]).astype(BF16)
    dest_here = lax.dynamic_slice_in_dim(pack_dest, seq_index, 1, 1)[:, 0]
    owners = jnp.arange(seq_count, dtype=jnp.int32)
    send_onehot = (dest_here[None, :] // slot_count == owners[:, None]) & (dest_here[None, :] >= 0)
    summ_send = mm(send_onehot.astype(BF16), summary).astype(BF16)
    summ_send = jnp.pad(summ_send.reshape(seq_count, RQ, ROW // RQ), ((0, 0), (0, 0), (0, 128 - ROW // RQ)))

    cache_t = jnp.swapaxes(latent_cache, 1, 2)
    keep_cols = keep_lists[:, 0, :].reshape(RQ, 2, seq_count).transpose(2, 0, 1)
    message = vmem_call(
        spread_kernel,
        pltpu.HBM((seq_count, 80, 128), BF16),
        [pltpu.VMEM((seq_count, 72, 128), BF16), pltpu.SemaphoreType.DMA],
        out_specs=APART,
    )(cache_t, keep_cols.reshape(seq_count * RQ, 2))

    live_f = jnp.broadcast_to(live_here.astype(F32)[:, None], (RQ, BLK))
    mask_f = live_f * kept_flag.astype(F32)
    part = vmem_call(
        attend_kernel,
        pltpu.HBM((seq_count, 40, 128), BF16),
        [
            pltpu.VMEM((H * RQ, LAT), F32),
            pltpu.VMEM((H * RQ, ROPE), F32),
            pltpu.VMEM(key_absorb.shape, BF16),
            pltpu.SemaphoreType.DMA((H,)),
        ],
        in_specs=[WHOLE, APART] + [WHOLE] * 6,
    )(
        query_all,
        key_absorb,
        cache_t,
        summary[:, :LAT],
        summary[:, LAT:],
        mask_f,
        live_f,
        summ_send,
    )
    part = lax.all_to_all(part, SEQ, 0, 0, tiled=True)

    half = (jnp.arange(RQ) // (RQ // 2) == seq_index % 2).astype(F32)
    message = vmem_call(
        merge_kernel,
        pltpu.HBM((seq_count, 80, 128), BF16),
        [
            pltpu.VMEM((seq_count, RQ, 128), BF16),
            pltpu.VMEM((LAT, VH), BF16),
            pltpu.SemaphoreType.DMA((2,)),
        ],
        in_specs=[SCALAR, WHOLE, APART, WHOLE, APART],
        out_specs=APART,
        input_output_aliases={4: 0},
    )(
        (seq_index // 2)[None],
        part,
        value_up,
        jnp.broadcast_to(half[:, None], (RQ, 128)),
        message,
    )
    values = lax.all_to_all(message, SEQ, 0, 0, tiled=True)
    slots = seq_index * slot_count + jnp.arange(slot_count, dtype=jnp.int32)
    summ_pick = jnp.any(pack_dest[None, :, :] == slots[:, None, None], axis=1)
    packed_summary = jnp.einsum(
        "js,sab->jab",
        summ_pick.astype(BF16),
        part[:, 32:40, : ROW // RQ],
        preferred_element_type=F32,
    )
    packed_summary = packed_summary.astype(BF16).reshape(slot_count, ROW)

    col_width = out_weight.shape[1]
    residual = lax.dynamic_slice_in_dim(hidden_in, seq_index * col_width, col_width, 1)
    out_t = out_weight.T
    side = (jnp.arange(2 * col_width) // col_width == seq_index % 2).astype(F32)
    hidden_send, own = vmem_call(
        hidden_kernel,
        (
            pltpu.HBM((seq_count, 48, 128), BF16),
            jax.ShapeDtypeStruct((RQ, 2 * col_width), BF16),
        ),
    )(
        values,
        jnp.concatenate([out_t, out_t], axis=0),
        jnp.concatenate([residual, residual], axis=1),
        jnp.broadcast_to(side[None, :], (RQ, 2 * col_width)),
        pack_dest.T.reshape(1, -1),
    )
    hidden_out = own[:, :col_width]
    hidden_all = lax.all_to_all(hidden_send, SEQ, 0, 0, tiled=True)
    packed_rows = vmem_call(settle_kernel, jax.ShapeDtypeStruct((slot_count, KB, ROW), BF16))(
        hidden_all
    )
    normed, norms = vmem_call(
        norm_kernel,
        (
            pltpu.HBM((mp_count, RQ, WIDE), BF16),
            jax.ShapeDtypeStruct((RQ, 128), F32),
        ),
    )(hidden_all, final_gain[None, :])
    state_norm = norms[:, 0]
    normed = lax.all_to_all(normed, MP, 0, 0, tiled=True)

    vocab_width = head_weight.shape[1]
    start = (seq_index * mp_count + mp_index) * vocab_width
    tenant_onehot = (tenant_ids[:, None] == jnp.arange(TENANTS, dtype=jnp.int32)[None, :]).astype(
        jnp.int32
    )
    window_low = jnp.sum(tenant_onehot * tenant_ranges[None, :, 0], axis=1) - start
    window_high = jnp.sum(tenant_onehot * tenant_ranges[None, :, 1], axis=1) - start
    best = vmem_call(top_kernel, pltpu.HBM((seq_count, mp_count, 128), F32))(
        normed, head_weight.T, window_low[:, None], window_high[:, None]
    )
    best = lax.all_to_all(best.reshape(seq_count * mp_count, 1, 128), ALL, 0, 0, tiled=True)
    top_logit = jnp.max(best[:, 0, :], axis=0)[:RQ]
    return (packed_rows, packed_summary, hidden_out, state_norm, top_logit)


def solution(mesh):
    seq_count, mp_count = mesh.devices.shape
    split = Mesh(
        mesh.devices.reshape(4, seq_count // 4, mp_count // 2, 2), ("sx", "sz", "y", "c")
    )
    in_specs = (
        P(MP, None),
        P(None, SEQ),
        P(),
        P(),
        P(None, SEQ),
        P(MP, SEQ, None),
        P(MP),
        P(MP, SEQ, None),
        P(MP, SEQ),
        P(MP, None),
        P(),
        P(None, ALL),
        P(),
        P(),
    )
    out_specs = (
        P(ALL, None, None),
        P(ALL, None),
        P(MP, SEQ),
        P(MP),
        P(MP),
    )
    return jax.shard_map(body, mesh=split, in_specs=in_specs, out_specs=out_specs, check_vma=False)
```

time: 445 us -> 133 us (0.30)
  blocking collectives: 297 us -> 0 us
  local copies, waits for them, and re-layouts: 45.3 us -> 9.26 us
  starting transfers between devices: 17.2 us -> 48.9 us
  Pallas kernels: 0 us -> 15.4 us
  between operations: 14.5 us -> 0.94 us
  matrix products: 11.5 us -> 2.94 us
  other arithmetic: 11.5 us -> 4.3 us
  waiting for transfers between devices: 45.7 us -> 50.6 us
    all_gather x4 -> x0, blocking collectives: 223 us -> none  [the longest x1 88.3 us: body(): lax.all_gather(query_part, 'seq', axis=1, tiled=True)]
    pmax x1 -> x0, blocking collectives: 74.2 us -> none  [body(): best_all = lax.pmax(local_best, ('seq', 'mp'))]
    all_to_all x2 -> x6, waiting for transfers between devices: 4.13 us -> 50.6 us  [the longest x1 14.3 us: body(): values = lax.all_to_all(message, SEQ, 0, 0, tiled=True)]
    all_gather x1 -> x0, waiting for transfers between devices: 41.6 us -> none  [merged(): everything = jax.tree.map(lambda part: lax.all_gather(part, axis), x)]
    all_to_all x2 -> x6, starting transfers between devices: 17.2 us -> 48.9 us  [the longest x1 11.9 us: body(): lax.all_to_all(jnp.broadcast_to(query_part[None], (seq_count, RQ, 128)),...]
    dynamic_slice x33 -> x1, local copies, waits for them, and re-layouts: 31.4 us -> 0.76 us  [body(): lax.dynamic_slice_in_dim(hidden_in, seq_index * col_width, col_width, 1)]
    pallas_call x0 -> x7, Pallas kernels: none -> 15.4 us  [the longest x1 7.12 us: body(): vmem_call(attend_kernel, pltpu.HBM((seq_count, 40, 128), BF16), [pltpu.VM...]
    dot_general x14 -> x4, matrix products: 11.5 us -> 2.94 us  [the longest x1 1.71 us: body(): jnp.einsum('nt,ntc->nc', weights_dropped, latent_cache, preferred_element...]
  transfers between devices with their start and end apart: 3 -> 6, of which waited for: 2 -> 6; matrix products, arithmetic and copies ran while one was open for 2% -> 7% of each run, Pallas kernels for 0% -> 3%
where the time goes in v1:
time: 133 us; the launch traced here: 132 us
  waiting for transfers between devices  50.6 us (38%)
  starting transfers between devices  48.9 us (37%)
  Pallas kernels  15.4 us (12%)
  local copies, waits for them, and re-layouts  9.26 us (7%)
  other arithmetic  4.3 us (3%)
  matrix products  2.94 us (2%)
    all_to_all x1, waiting for transfers between devices, body(): values = lax.all_to_all(message, SEQ, 0, 0, tiled=True)  14.3 us
    all_to_all x1, starting transfers between devices, body(): lax.all_to_all(jnp.broadcast_to(query_part[None], (seq_count, RQ, 128)),...  11.9 us
    all_to_all x1, starting transfers between devices, body(): normed = lax.all_to_all(normed, MP, 0, 0, tiled=True)  10.4 us
    all_to_all x1, waiting for transfers between devices, body(): lax.all_to_all(best.reshape(seq_count * mp_count, 1, 128), ALL, 0, 0, til...  10.3 us
    all_to_all x1, waiting for transfers between devices, body(): hidden_all = lax.all_to_all(hidden_send, SEQ, 0, 0, tiled=True)  10.1 us
    all_to_all x1, starting transfers between devices, body(): hidden_all = lax.all_to_all(hidden_send, SEQ, 0, 0, tiled=True)  7.74 us
    pallas_call x1, Pallas kernels, body(): vmem_call(attend_kernel, pltpu.HBM((seq_count, 40, 128), BF16), [pltpu.VM...  7.12 us
    all_to_all x1, starting transfers between devices, body(): values = lax.all_to_all(message, SEQ, 0, 0, tiled=True)  6.92 us
  transfers between devices with their start and end apart: 6, of which 6 were waited for; matrix products, arithmetic and copies ran while one was open for 7% of the time, Pallas kernels for 3%

profile of v1, /device:TPU:1, one launch (start us, length us, event | category | flops | bytes accessed | tf_op | source)
XLA Modules:
  0.0 132.3 jit_solution(15528158652023358939)
XLA Ops:
  0.6 0.0 copy-start
  0.6 0.0 copy-start.1
  0.7 1.0 copy-done
  1.6 1.0 convolution_convert_fusion.2
  2.6 0.1 pad_slice_fusion
  2.7 0.1 maximum_select_fusion
  2.7 0.7 broadcast_in_dim.13
  3.4 11.9 %all-to-all-start = ((bf16[32,8,128]{2,1,0:T(8,128)(2,1)}), bf16[32,8,128]{2,1,0:T(8,128)(2,1)S(1)}, u32[]{:S(2)}, u32[]{:S(2)}) async-start(bf16[32,8,128]{2,1,0:T(8,128)(2,1)} %broadcast_in_dim.13), calls=%async_computation | async-start | bytes 131072 | tf_op jit(solution)/shard_map/all_to_all | solution.py:321
  15.3 0.9 dynamic-slice_reduce_fusion
  16.2 0.8 convert_reduce_fusion
  17.0 0.7 compare_convert_fusion.2
  17.7 0.9 convert_reduce_fusion.1
  18.5 1.7 %fusion.6 = f32[8,1,576]{2,1,0:T(1,128)S(1)} fusion(bf16[8,128,576]{1,2,0:T(8,128)(2,1)} %param.19, bf16[8,128,1]{1,0,2:T(8,128)(2,1)S(1)} %bitcast.43), kind=kOutput, calls=%fused_computation.14 | convolution fusion | flops 1179648 | bytes 1200128 | tf_op jit(solution)/shard_map/nt,ntc->nc/dot_general | solution.py:331
  20.2 0.1 fusion.1
  20.3 0.1 convolution_convert_fusion
  20.5 0.1 reshape.151
  20.6 3.5 %all-to-all-done.query_ref = bf16[32,8,128]{2,1,0:T(8,128)(2,1)S(1)} async-done(((bf16[32,8,128]{2,1,0:T(8,128)(2,1)}), bf16[32,8,128]{2,1,0:T(8,128)(2,1)S(1)}, u32[]{:S(2)}, u32[]{:S(2)}) %all-to-all-start) | async-done | bytes 65568 | tf_op jit(solution)/shard_map/all_to_all | solution.py:321
  24.1 0.1 broadcast_in_dim.14.live_ref
  24.2 0.0 copy-done.1
  24.2 1.6 %copy-done.2 = bf16[16,128,512]{2,1,0:T(8,128)(2,1)S(1)} copy-done((bf16[16,128,512]{2,1,0:T(8,128)(2,1)S(1)}, bf16[16,128,512]{2,1,0:T(8,128)(2,1)}, u32[]{:S(2)}) %copy-start.2) | copy-done | bytes 2097176
  25.8 7.1 %shard_map.173 = bf16[32,40,128]{2,1,0:T(8,128)(2,1)} custom-call(bf16[32,8,128]{2,1,0:T(8,128)(2,1)S(1)} %all-to-all-done.query_ref, bf16[16,128,512]{2,1,0:T(8,128)(2,1)S(1)} %copy-done.2, bf16[8,576,128]{2,1,0:T(8,128)(2,1)S(1)} %bitcast.35, bf16[8,512]{1,0:T(8,128)(2,1)S(1)} %slice.43.summ_ref, bf16[8,64]{1,0:T(8,128)(2,1)S(1)} %slice.44.summ_tail_ref, ...), custom_call_target="tpu_custom_call" | custom-call | tf_op jit(solution)/shard_map/pallas_call | solution.py:350
  32.9 5.7 %all-to-all-start.1 = ((bf16[32,40,128]{2,1,0:T(8,128)(2,1)}), bf16[32,40,128]{2,1,0:T(8,128)(2,1)S(1)}, u32[]{:S(2)}, u32[]{:S(2)}) async-start(bf16[32,40,128]{2,1,0:T(8,128)(2,1)} %shard_map.173), calls=%async_computation.1 | async-start | bytes 655360 | tf_op jit(solution)/shard_map/all_to_all | solution.py:370
  38.7 0.5 broadcast.176
  39.2 0.7 reduce.8
  39.9 0.1 reshape_squeeze.3
  39.9 0.1 copy.38
  40.1 2.4 %shard_map.174.before_ref = bf16[32,80,128]{2,1,0:T(8,128)(2,1)} custom-call(bf16[8,576,128]{2,1,0:T(8,128)(2,1)S(1)} %bitcast.36, s32[256,2]{1,0:T(8,128)S(1)} %bitcast.38), custom_call_target="tpu_custom_call" | custom-call | tf_op jit(solution)/shard_map/pallas_call | solution.py:341
  42.5 6.2 %all-to-all-done.1.parts_ref = bf16[32,40,128]{2,1,0:T(8,128)(2,1)S(1)} async-done(((bf16[32,40,128]{2,1,0:T(8,128)(2,1)}), bf16[32,40,128]{2,1,0:T(8,128)(2,1)S(1)}, u32[]{:S(2)}, u32[]{:S(2)}) %all-to-all-start.1) | async-done | bytes 327712 | tf_op jit(solution)/shard_map/all_to_all | solution.py:370
  48.7 0.1 broadcast_in_dim.15.half_ref
  48.8 1.6 %copy-done.3 = bf16[16,512,128]{2,1,0:T(8,128)(2,1)S(1)} copy-done((bf16[16,512,128]{2,1,0:T(8,128)(2,1)S(1)}, bf16[16,512,128]{2,1,0:T(8,128)(2,1)}, u32[]{:S(2)}) %copy-start.3) | copy-done | bytes 2097176
  50.4 1.2 shard_map.175
  51.6 0.0 copy-start.6
  51.6 0.0 copy-start.5
  51.6 6.9 %all-to-all-start.2 = ((bf16[32,80,128]{2,1,0:T(8,128)(2,1)}), bf16[32,80,128]{2,1,0:T(8,128)(2,1)S(1)}, u32[]{:S(2)}, u32[]{:S(2)}) async-start(bf16[32,80,128]{2,1,0:T(8,128)(2,1)} %shard_map.175), calls=%async_computation.2 | async-start | bytes 1310720 | tf_op jit(solution)/shard_map/all_to_all | solution.py:391
  58.5 0.0 copy-done.6
  58.5 0.1 copy.39
  58.6 0.1 reshape.153.dest_ref
  58.7 0.8 constant_dynamic-slice_fusion
  59.5 0.1 pad_maximum_fusion.1.residual_ref
  59.5 0.0 copy-done.5
  59.6 0.0 copy-start.8
  59.6 0.0 copy-start.9
  59.6 0.0 copy-start.10
  59.6 14.3 %all-to-all-done.2.parts_ref = bf16[32,80,128]{2,1,0:T(8,128)(2,1)S(1)} async-done(((bf16[32,80,128]{2,1,0:T(8,128)(2,1)}), bf16[32,80,128]{2,1,0:T(8,128)(2,1)S(1)}, u32[]{:S(2)}, u32[]{:S(2)}) %all-to-all-start.2) | async-done | bytes 655392 | tf_op jit(solution)/shard_map/all_to_all | solution.py:391
  73.9 1.3 %shard_map.176 = (bf16[32,48,128]{2,1,0:T(8,128)(2,1)}, bf16[8,128]{1,0:T(8,128)(2,1)}) custom-call(bf16[32,80,128]{2,1,0:T(8,128)(2,1)S(1)} %all-to-all-done.2.parts_ref, bf16[128,2048]{1,0:T(8,128)(2,1)S(1)} %pad_maximum_fusion.weight_ref, bf16[8,128]{1,0:T(8,128)(2,1)S(1)} %pad_maximum_fusion.1.residual_ref, f32[8,128]{1,0:T(8,128)S(1)} %broadcast_in_dim.16.side_ref, ...), custom_call_target="tpu_custom_call" | custom-call | tf_op jit(solution)/shard_map/pallas_call | solution.py:406
  75.3 7.7 %all-to-all-start.3 = ((bf16[32,48,128]{2,1,0:T(8,128)(2,1)}), bf16[32,48,128]{2,1,0:T(8,128)(2,1)S(1)}, u32[]{:S(2)}, u32[]{:S(2)}) async-start(bf16[32,48,128]{2,1,0:T(8,128)(2,1)} %get-tuple-element.9), calls=%async_computation.3 | async-start | bytes 786432 | tf_op jit(solution)/shard_map/all_to_all | solution.py:420
  83.1 0.0 copy-done.9
  83.1 0.1 select_reduce_fusion
  83.2 10.1 %all-to-all-done.3.parts_ref = bf16[32,48,128]{2,1,0:T(8,128)(2,1)S(1)} async-done(((bf16[32,48,128]{2,1,0:T(8,128)(2,1)}), bf16[32,48,128]{2,1,0:T(8,128)(2,1)S(1)}, u32[]{:S(2)}, u32[]{:S(2)}) %all-to-all-start.3) | async-done | bytes 393248 | tf_op jit(solution)/shard_map/all_to_all | solution.py:420
  93.3 0.8 shard_map.178
  94.1 10.4 %all-to-all-start.4 = ((bf16[8,8,2048]{2,1,0:T(8,128)(2,1)}), bf16[8,8,2048]{2,1,0:T(8,128)(2,1)S(1)}, u32[]{:S(2)}, u32[]{:S(2)}) async-start(bf16[8,8,2048]{2,1,0:T(8,128)(2,1)} %get-tuple-element.12), calls=%async_computation.4 | async-start | bytes 524288 | tf_op jit(solution)/shard_map/all_to_all | solution.py:432
  104.5 0.1 copy.43.high_ref
  104.6 0.1 copy.42.low_ref
  104.7 0.1 compare_reduce_fusion
  104.8 6.2 %all-to-all-done.4.rows_ref = bf16[8,8,2048]{2,1,0:T(8,128)(2,1)S(1)} async-done(((bf16[8,8,2048]{2,1,0:T(8,128)(2,1)}), bf16[8,8,2048]{2,1,0:T(8,128)(2,1)S(1)}, u32[]{:S(2)}, u32[]{:S(2)}) %all-to-all-start.4) | async-done | bytes 262176 | tf_op jit(solution)/shard_map/all_to_all | solution.py:432
  111.0 0.0 copy-done.4
  111.0 1.4 %shard_map.179 = f32[32,8,128]{2,1,0:T(8,128)} custom-call(bf16[8,8,2048]{2,1,0:T(8,128)(2,1)S(1)} %all-to-all-done.4.rows_ref, bf16[400,2048]{1,0:T(8,128)(2,1)S(1)} %bitcast.37, s32[64,1]{1,0:T(8,128)S(1)} %copy.42.low_ref, s32[64,1]{1,0:T(8,128)S(1)} %copy.43.high_ref), custom_call_target="tpu_custom_call" | custom-call | tf_op jit(solution)/shard_map/pallas_call | solution.py:441
  112.4 6.3 %all-to-all-start.5 = ((f32[256,1,128]{2,1,0:T(1,128)}), f32[256,1,128]{2,1,0:T(1,128)S(1)}, u32[]{:S(2)}, u32[]{:S(2)}) async-start(f32[256,1,128]{2,1,0:T(1,128)} %bitcast.39), calls=%async_computation.5 | async-start | bytes 262144 | tf_op jit(solution)/shard_map/all_to_all | solution.py:444
  118.7 0.1 convolution_convert_fusion.1
  118.8 0.7 reshape.154
  119.5 1.1 shard_map.177
  120.6 0.6 slice_reduce_fusion
  121.2 10.3 %all-to-all-done.5 = f32[256,1,128]{2,1,0:T(1,128)S(1)} async-done(((f32[256,1,128]{2,1,0:T(1,128)}), f32[256,1,128]{2,1,0:T(1,128)S(1)}, u32[]{:S(2)}, u32[]{:S(2)}) %all-to-all-start.5) | async-done | bytes 131104 | tf_op jit(solution)/shard_map/all_to_all | solution.py:444
  131.5 0.8 reduce_max.9
  (22 shorter events, 0.1 us)
Async XLA Ops:
  0.6 1.0 copy-start
  0.6 23.6 %copy-start.1 = (bf16[8,128,576]{1,2,0:T(8,128)(2,1)S(1)}, bf16[8,128,576]{1,2,0:T(8,128)(2,1)}, u32[]{:S(2)}) copy-start(bf16[8,128,576]{1,2,0:T(8,128)(2,1)} %param.19) | copy-start | bytes 3538948
  3.4 20.7 %all-to-all-start = ((bf16[32,8,128]{2,1,0:T(8,128)(2,1)}), bf16[32,8,128]{2,1,0:T(8,128)(2,1)S(1)}, u32[]{:S(2)}, u32[]{:S(2)}) async-start(bf16[32,8,128]{2,1,0:T(8,128)(2,1)} %broadcast_in_dim.13), calls=%async_computation | async-start | bytes 131072 | tf_op jit(solution)/shard_map/all_to_all | solution.py:321
  24.2 1.6 %copy-start.2 = (bf16[16,128,512]{2,1,0:T(8,128)(2,1)S(1)}, bf16[16,128,512]{2,1,0:T(8,128)(2,1)}, u32[]{:S(2)}) copy-start(bf16[16,128,512]{2,1,0:T(8,128)(2,1)} %absorb_ref.1) | copy-start | bytes 6291460
  25.8 13.4 %copy-start.7 = (s32[8,1,64]{2,1,0:T(1,128)S(1)}, s32[8,1,64]{2,1,0:T(1,128)}, u32[]{:S(2)}) copy-start(s32[8,1,64]{2,1,0:T(1,128)} %param.21) | copy-start | bytes 6148
  32.9 15.8 %all-to-all-start.1 = ((bf16[32,40,128]{2,1,0:T(8,128)(2,1)}), bf16[32,40,128]{2,1,0:T(8,128)(2,1)S(1)}, u32[]{:S(2)}, u32[]{:S(2)}) async-start(bf16[32,40,128]{2,1,0:T(8,128)(2,1)} %shard_map.173), calls=%async_computation.1 | async-start | bytes 655360 | tf_op jit(solution)/shard_map/all_to_all | solution.py:370
  48.8 1.6 %copy-start.3 = (bf16[16,512,128]{2,1,0:T(8,128)(2,1)S(1)}, bf16[16,512,128]{2,1,0:T(8,128)(2,1)}, u32[]{:S(2)}) copy-start(bf16[16,512,128]{2,1,0:T(8,128)(2,1)} %up_ref.1) | copy-start | bytes 6291460
  51.6 7.0 %copy-start.6 = (s32[8,32]{1,0:T(8,128)S(1)}, s32[8,32]{1,0:T(8,128)}, u32[]{:S(2)}) copy-start(s32[8,32]{1,0:T(8,128)} %param.23) | copy-start | bytes 3076
  51.6 8.0 %copy-start.5 = (bf16[2048,64]{0,1:T(8,128)(2,1)S(1)}, bf16[2048,64]{0,1:T(8,128)(2,1)}, u32[]{:S(2)}) copy-start(bf16[2048,64]{0,1:T(8,128)(2,1)} %param.18) | copy-start | bytes 786436
  51.6 22.3 %all-to-all-start.2 = ((bf16[32,80,128]{2,1,0:T(8,128)(2,1)}), bf16[32,80,128]{2,1,0:T(8,128)(2,1)S(1)}, u32[]{:S(2)}, u32[]{:S(2)}) async-start(bf16[32,80,128]{2,1,0:T(8,128)(2,1)} %shard_map.175), calls=%async_computation.2 | async-start | bytes 1310720 | tf_op jit(solution)/shard_map/all_to_all | solution.py:391
  59.6 23.4 %copy-start.8 = (bf16[2048]{0:T(1024)(128)(2,1)S(1)}, bf16[2048]{0:T(1024)(128)(2,1)}, u32[]{:S(2)}) copy-start(bf16[2048]{0:T(1024)(128)(2,1)} %param.24) | copy-start | bytes 12292
  59.6 23.5 %copy-start.9 = (s32[4,2]{0,1:T(2,128)S(1)}, s32[4,2]{0,1:T(2,128)}, u32[]{:S(2)}) copy-start(s32[4,2]{0,1:T(2,128)} %param.26) | copy-start | bytes 100
  59.6 23.5 %copy-start.10 = (s32[64]{0:T(128)S(1)}, s32[64]{0:T(128)}, u32[]{:S(2)}) copy-start(s32[64]{0:T(128)} %param.27) | copy-start | bytes 772
  75.3 35.8 %copy-start.4 = (bf16[2048,400]{0,1:T(8,128)(2,1)S(1)}, bf16[2048,400]{0,1:T(8,128)(2,1)}, u32[]{:S(2)}) copy-start(bf16[2048,400]{0,1:T(8,128)(2,1)} %param.25) | copy-start | bytes 4915204
  75.3 18.0 %all-to-all-start.3 = ((bf16[32,48,128]{2,1,0:T(8,128)(2,1)}), bf16[32,48,128]{2,1,0:T(8,128)(2,1)S(1)}, u32[]{:S(2)}, u32[]{:S(2)}) async-start(bf16[32,48,128]{2,1,0:T(8,128)(2,1)} %get-tuple-element.9), calls=%async_computation.3 | async-start | bytes 786432 | tf_op jit(solution)/shard_map/all_to_all | solution.py:420
  94.1 16.9 %all-to-all-start.4 = ((bf16[8,8,2048]{2,1,0:T(8,128)(2,1)}), bf16[8,8,2048]{2,1,0:T(8,128)(2,1)S(1)}, u32[]{:S(2)}, u32[]{:S(2)}) async-start(bf16[8,8,2048]{2,1,0:T(8,128)(2,1)} %get-tuple-element.12), calls=%async_computation.4 | async-start | bytes 524288 | tf_op jit(solution)/shard_map/all_to_all | solution.py:432
  112.4 19.1 %all-to-all-start.5 = ((f32[256,1,128]{2,1,0:T(1,128)}), f32[256,1,128]{2,1,0:T(1,128)S(1)}, u32[]{:S(2)}, u32[]{:S(2)}) async-start(f32[256,1,128]{2,1,0:T(1,128)} %bitcast.39), calls=%async_computation.5 | async-start | bytes 262144 | tf_op jit(solution)/shard_map/all_to_all | solution.py:444

commit v2 on v1

--- a/solution.py
+++ b/solution.py
@@ -63,7 +63,23 @@
     return (high, middle, rest - middle)
 
 
-def spread_kernel(cache_ref, keep_ref, message_ref, out_ref, sem):
+def query_kernel(side_ref, hidden_ref, weight_ref, out_ref, hidden_here, weight_here, sems):
+    first = pltpu.make_async_copy(hidden_ref, hidden_here, sems.at[0])
+    second = pltpu.make_async_copy(weight_ref, weight_here, sems.at[1])
+    first.start()
+    second.start()
+    first.wait()
+    second.wait()
+    query = mm_nt(hidden_here[...], weight_here[...]).astype(BF16).astype(F32)
+    query = jnp.concatenate([query, jnp.zeros((RQ, 128 - HALF), F32)], axis=1)
+    query = jnp.where(side_ref[0] == 0, query, pltpu.roll(query, HALF, 1)).astype(BF16)
+    for d in range(out_ref.shape[0]):
+        out_ref[d] = query
+
+
+def spread_kernel(head_ref, cache_ref, keep_ref, up_ref, message_ref, up_here, out_ref, sems):
+    fetch = pltpu.make_async_copy(up_ref.at[head_ref[0]], up_here, sems.at[1])
+    fetch.start()
     rows = out_ref.shape[0] * RQ
     lane = iota((rows, BLK), 1)
     request = iota((rows, BLK), 0) % RQ
@@ -87,9 +103,10 @@
                 ].astype(BF16)
     for i in range(out_ref.shape[0]):
         out_ref[i, 64:72, :] = tail[RQ * i : RQ * i + RQ, :].astype(BF16)
-    copy = pltpu.make_async_copy(out_ref, message_ref.at[:, RQ:, :], sem)
+    copy = pltpu.make_async_copy(out_ref, message_ref.at[:, RQ:, :], sems.at[0])
     copy.start()
     copy.wait()
+    fetch.wait()
 
 
 def attend_kernel(
@@ -107,13 +124,17 @@
     absorb_here,
     sems,
 ):
-    copies = [
-        pltpu.make_async_copy(absorb_ref.at[h], absorb_here.at[h], sems.at[h]) for h in range(H)
-    ]
+    parts = sems.shape[0]
+    step = H // parts
+    copies = []
+    for k in range(parts):
+        cut = slice(step * k, step * k + step)
+        copies.append(pltpu.make_async_copy(absorb_ref.at[cut], absorb_here.at[cut], sems.at[k]))
     for copy in copies:
         copy.start()
     for h in range(H):
-        copies[h].wait()
+        if h % step == 0:
+            copies[h // step].wait()
         first = query_ref[2 * h].astype(F32)
         second = query_ref[2 * h + 1].astype(F32)
         nope = jnp.where(iota(first.shape, 1) < HALF, first, second).astype(BF16)
@@ -178,9 +199,7 @@
             out_ref[d, 32:40, :] = (sides[half][cut] + summ_send_ref[d].astype(F32)).astype(BF16)
 
 
-def merge_kernel(head_ref, parts_ref, up_ref, half_ref, before_ref, message_ref, out_ref, up_here, sems):
-    fetch = pltpu.make_async_copy(up_ref.at[head_ref[0]], up_here, sems.at[0])
-    fetch.start()
+def merge_kernel(parts_ref, up_ref, half_ref, before_ref, message_ref, out_ref, sem):
     count = parts_ref.shape[0]
     sides = []
     for i in range(count):
@@ -199,12 +218,11 @@
             column = column + factors[i] * block
         column = column + pltpu.roll(column, RQ // 2, 0)
         attended.append((column / total).astype(BF16))
-    fetch.wait()
-    values = mm(jnp.concatenate(attended, axis=1), up_here[...])
+    values = mm(jnp.concatenate(attended, axis=1), up_ref[...])
     values = jnp.where(half_ref[...] > 0.0, values, 0.0).astype(BF16)
     for d in range(out_ref.shape[0]):
         out_ref[d] = values
-    copy = pltpu.make_async_copy(out_ref, message_ref.at[:, :RQ, :], sems.at[1])
+    copy = pltpu.make_async_copy(out_ref, message_ref.at[:, :RQ, :], sem)
     copy.start()
     copy.wait()
 
@@ -315,12 +333,21 @@
     mp_index = lax.axis_index(MP)
     slot_count = RQ // 2
 
-    query_part = mm(hidden_in, query_weight).astype(BF16)
-    query_part = jnp.pad(query_part, ((0, 0), (0, 128 - HALF)))
-    query_part = jnp.where(seq_index % 2 == 0, query_part, jnp.roll(query_part, HALF, axis=1))
-    query_all = lax.all_to_all(
-        jnp.broadcast_to(query_part[None], (seq_count, RQ, 128)), SEQ, 0, 0, tiled=True
-    )
+    query_send = vmem_call(
+        query_kernel,
+        pltpu.HBM((seq_count, RQ, 128), BF16),
+        [
+            pltpu.VMEM(hidden_in.shape, BF16),
+            pltpu.VMEM(query_weight.shape[::-1], BF16),
+            pltpu.SemaphoreType.DMA((2,)),
+        ],
+        in_specs=[SCALAR, APART, APART],
+    )(
+        (seq_index % 2)[None],
+        pltpu.with_memory_space_constraint(hidden_in, pltpu.HBM),
+        pltpu.with_memory_space_constraint(query_weight.T, pltpu.HBM),
+    )
+    query_all = lax.all_to_all(query_send, SEQ, 0, 0, tiled=True)
 
     positions = jnp.arange(BLK, dtype=jnp.int32)
     keep_onehot = keep_lists[:, 0, :, None] == positions[None, None, :]
@@ -338,12 +365,18 @@
 
     cache_t = jnp.swapaxes(latent_cache, 1, 2)
     keep_cols = keep_lists[:, 0, :].reshape(RQ, 2, seq_count).transpose(2, 0, 1)
-    message = vmem_call(
+    message, up_here = vmem_call(
         spread_kernel,
-        pltpu.HBM((seq_count, 80, 128), BF16),
-        [pltpu.VMEM((seq_count, 72, 128), BF16), pltpu.SemaphoreType.DMA],
-        out_specs=APART,
-    )(cache_t, keep_cols.reshape(seq_count * RQ, 2))
+        (pltpu.HBM((seq_count, 80, 128), BF16), pltpu.VMEM((LAT, VH), BF16)),
+        [pltpu.VMEM((seq_count, 72, 128), BF16), pltpu.SemaphoreType.DMA((2,))],
+        in_specs=[SCALAR, WHOLE, WHOLE, APART],
+        out_specs=(APART, WHOLE),
+    )(
+        (seq_index // 2)[None],
+        cache_t,
+        keep_cols.reshape(seq_count * RQ, 2),
+        pltpu.with_memory_space_constraint(value_up, pltpu.HBM),
+    )
 
     live_f = jnp.broadcast_to(live_here.astype(F32)[:, None], (RQ, BLK))
     mask_f = live_f * kept_flag.astype(F32)
@@ -354,12 +387,12 @@
             pltpu.VMEM((H * RQ, LAT), F32),
             pltpu.VMEM((H * RQ, ROPE), F32),
             pltpu.VMEM(key_absorb.shape, BF16),
-            pltpu.SemaphoreType.DMA((H,)),
+            pltpu.SemaphoreType.DMA((4,)),
         ],
         in_specs=[WHOLE, APART] + [WHOLE] * 6,
     )(
         query_all,
-        key_absorb,
+        pltpu.with_memory_space_constraint(key_absorb, pltpu.HBM),
         cache_t,
         summary[:, :LAT],
         summary[:, LAT:],
@@ -375,16 +408,14 @@
         pltpu.HBM((seq_count, 80, 128), BF16),
         [
             pltpu.VMEM((seq_count, RQ, 128), BF16),
-            pltpu.VMEM((LAT, VH), BF16),
-            pltpu.SemaphoreType.DMA((2,)),
+            pltpu.SemaphoreType.DMA,
         ],
-        in_specs=[SCALAR, WHOLE, APART, WHOLE, APART],
+        in_specs=[WHOLE, WHOLE, WHOLE, APART],
         out_specs=APART,
-        input_output_aliases={4: 0},
+        input_output_aliases={3: 0},
     )(
-        (seq_index // 2)[None],
         part,
-        value_up,
+        pltpu.with_memory_space_constraint(up_here, pltpu.VMEM),
         jnp.broadcast_to(half[:, None], (RQ, 128)),
         message,
     )
@@ -442,7 +473,7 @@
         normed, head_weight.T, window_low[:, None], window_high[:, None]
     )
     best = lax.all_to_all(best.reshape(seq_count * mp_count, 1, 128), ALL, 0, 0, tiled=True)
-    top_logit = jnp.max(best[:, 0, :], axis=0)[:RQ]
+    top_logit = jnp.max(best.reshape(seq_count, mp_count, 128), axis=(0, 1))[:RQ]
     return (packed_rows, packed_summary, hidden_out, state_norm, top_logit)
 
 

time: 133 us -> 126 us (0.947)
  local copies, waits for them, and re-layouts: 9.26 us -> 4.38 us
    unnamed x23 -> x17, local copies, waits for them, and re-layouts: 4.7 us -> 0.55 us
    pallas_call x1, Pallas kernels: 7.12 us -> 3.99 us  [body(): vmem_call(attend_kernel, pltpu.HBM((seq_count, 40, 128), BF16), [pltpu.VM...]
    pallas_call x1 -> x2, Pallas kernels: 2.4 us -> 4.45 us  [the longest x1 2.4 us: body(): vmem_call(spread_kernel, (pltpu.HBM((seq_count, 80, 128), BF16), pltpu.VM...]
  transfers between devices with their start and end apart: 6 -> 6, of which waited for: 6 -> 6; matrix products, arithmetic and copies ran while one was open for 7% -> 8% of each run, Pallas kernels for 3% -> 3%
where the time goes in v2:
time: 126 us; the launch traced here: 125 us
  waiting for transfers between devices  50.6 us (40%)
  starting transfers between devices  48.8 us (39%)
  Pallas kernels  14.1 us (11%)
  local copies, waits for them, and re-layouts  4.38 us (3%)
  other arithmetic  4.22 us (3%)
  matrix products  1.98 us (2%)
    all_to_all x1, waiting for transfers between devices, body(): values = lax.all_to_all(message, SEQ, 0, 0, tiled=True)  14.3 us
    all_to_all x1, starting transfers between devices, body(): query_all = lax.all_to_all(query_send, SEQ, 0, 0, tiled=True)  11.9 us
    all_to_all x1, starting transfers between devices, body(): normed = lax.all_to_all(normed, MP, 0, 0, tiled=True)  10.4 us
    all_to_all x1, waiting for transfers between devices, body(): lax.all_to_all(best.reshape(seq_count * mp_count, 1, 128), ALL, 0, 0, til...  10.3 us
    all_to_all x1, waiting for transfers between devices, body(): hidden_all = lax.all_to_all(hidden_send, SEQ, 0, 0, tiled=True)  10.1 us
    all_to_all x1, starting transfers between devices, body(): hidden_all = lax.all_to_all(hidden_send, SEQ, 0, 0, tiled=True)  7.74 us
    all_to_all x1, starting transfers between devices, body(): values = lax.all_to_all(message, SEQ, 0, 0, tiled=True)  6.78 us
    all_to_all x1, starting transfers between devices, body(): lax.all_to_all(best.reshape(seq_count * mp_count, 1, 128), ALL, 0, 0, til...  6.28 us
  transfers between devices with their start and end apart: 6, of which 6 were waited for; matrix products, arithmetic and copies ran while one was open for 8% of the time, Pallas kernels for 3%

profile of v2, /device:TPU:1, one launch (start us, length us, event | category | flops | bytes accessed | tf_op | source)
XLA Modules:
  0.0 125.0 jit_solution(9962370418153146582)
XLA Ops:
  0.6 0.0 copy-start
  0.7 2.0 %shard_map.173 = bf16[32,8,128]{2,1,0:T(8,128)(2,1)} custom-call(s32[1]{0:T(128)} %bitcast.side_ref, bf16[8,2048]{1,0:T(8,128)(2,1)} %hidden_ref.1, bf16[96,2048]{1,0:T(8,128)(2,1)} %bitcast.39), custom_call_target="tpu_custom_call" | custom-call | tf_op jit(solution)/shard_map/pallas_call | solution.py:336
  2.7 11.9 %all-to-all-start = ((bf16[32,8,128]{2,1,0:T(8,128)(2,1)}), bf16[32,8,128]{2,1,0:T(8,128)(2,1)S(1)}, u32[]{:S(2)}, u32[]{:S(2)}) async-start(bf16[32,8,128]{2,1,0:T(8,128)(2,1)} %shard_map.173), calls=%async_computation | async-start | bytes 131072 | tf_op jit(solution)/shard_map/all_to_all | solution.py:350
  14.6 0.9 dynamic-slice_reduce_fusion
  15.5 0.8 convert_reduce_fusion
  16.3 0.7 compare_convert_fusion.2
  17.0 0.9 convert_reduce_fusion.1
  17.9 1.7 %fusion.6 = f32[8,1,576]{2,1,0:T(1,128)S(1)} fusion(bf16[8,128,576]{1,2,0:T(8,128)(2,1)} %param.19, bf16[8,128,1]{1,0,2:T(8,128)(2,1)S(1)} %bitcast.42), kind=kOutput, calls=%fused_computation.13 | convolution fusion | flops 1179648 | bytes 1200128 | tf_op jit(solution)/shard_map/nt,ntc->nc/dot_general | solution.py:358
  19.6 0.1 fusion.1
  19.7 0.1 convolution_convert_fusion
  19.8 0.1 reshape.151
  19.9 3.5 %all-to-all-done.query_ref = bf16[32,8,128]{2,1,0:T(8,128)(2,1)S(1)} async-done(((bf16[32,8,128]{2,1,0:T(8,128)(2,1)}), bf16[32,8,128]{2,1,0:T(8,128)(2,1)S(1)}, u32[]{:S(2)}, u32[]{:S(2)}) %all-to-all-start) | async-done | bytes 65568 | tf_op jit(solution)/shard_map/all_to_all | solution.py:350
  23.5 0.1 broadcast_in_dim.13.live_ref
  23.5 0.0 copy-done
  23.5 0.0 copy-start.4
  23.5 4.0 %shard_map.174 = bf16[32,40,128]{2,1,0:T(8,128)(2,1)} custom-call(bf16[32,8,128]{2,1,0:T(8,128)(2,1)S(1)} %all-to-all-done.query_ref, bf16[16,128,512]{2,1,0:T(8,128)(2,1)} %absorb_ref.1, bf16[8,576,128]{2,1,0:T(8,128)(2,1)S(1)} %bitcast.34, bf16[8,512]{1,0:T(8,128)(2,1)S(1)} %slice.32.summ_ref, bf16[8,64]{1,0:T(8,128)(2,1)S(1)} %slice.33.summ_tail_ref, ...), custom_call_target="tpu_custom_call" | custom-call | tf_op jit(solution)/shard_map/pallas_call | solution.py:383
  27.5 5.7 %all-to-all-start.1 = ((bf16[32,40,128]{2,1,0:T(8,128)(2,1)}), bf16[32,40,128]{2,1,0:T(8,128)(2,1)S(1)}, u32[]{:S(2)}, u32[]{:S(2)}) async-start(bf16[32,40,128]{2,1,0:T(8,128)(2,1)} %shard_map.174), calls=%async_computation.1 | async-start | bytes 655360 | tf_op jit(solution)/shard_map/all_to_all | solution.py:403
  33.3 0.5 broadcast.173
  33.8 0.0 copy-done.4
  33.8 0.7 reduce.8
  34.5 0.1 reshape_squeeze.3
  34.6 0.1 copy.38
  34.7 2.4 %shard_map.175 = (bf16[32,80,128]{2,1,0:T(8,128)(2,1)}, bf16[512,128]{1,0:T(8,128)(2,1)S(1)}) custom-call(s32[1]{0:T(128)} %bitcast.6.head_ref, bf16[8,576,128]{2,1,0:T(8,128)(2,1)S(1)} %bitcast.35, s32[256,2]{1,0:T(8,128)S(1)} %bitcast.37, bf16[16,512,128]{2,1,0:T(8,128)(2,1)} %up_ref.1), custom_call_target="tpu_custom_call" | custom-call | tf_op jit(solution)/shard_map/pallas_call | solution.py:368
  37.1 6.2 %all-to-all-done.1.parts_ref = bf16[32,40,128]{2,1,0:T(8,128)(2,1)S(1)} async-done(((bf16[32,40,128]{2,1,0:T(8,128)(2,1)}), bf16[32,40,128]{2,1,0:T(8,128)(2,1)S(1)}, u32[]{:S(2)}, u32[]{:S(2)}) %all-to-all-start.1) | async-done | bytes 327712 | tf_op jit(solution)/shard_map/all_to_all | solution.py:403
  43.3 0.1 broadcast_in_dim.15.half_ref
  43.4 0.0 copy-start.3
  43.4 0.0 copy-start.2
  43.4 1.0 shard_map.176
  44.4 6.8 %all-to-all-start.2 = ((bf16[32,80,128]{2,1,0:T(8,128)(2,1)}), bf16[32,80,128]{2,1,0:T(8,128)(2,1)S(1)}, u32[]{:S(2)}, u32[]{:S(2)}) async-start(bf16[32,80,128]{2,1,0:T(8,128)(2,1)} %shard_map.176), calls=%async_computation.2 | async-start | bytes 1310720 | tf_op jit(solution)/shard_map/all_to_all | solution.py:422
  51.2 0.0 copy-done.3
  51.2 0.1 copy.39
  51.3 0.1 reshape.153.dest_ref
  51.4 0.8 constant_dynamic-slice_fusion
  52.2 0.1 pad_maximum_fusion.1.residual_ref
  52.2 0.0 copy-done.2
  52.3 0.0 copy-start.5
  52.3 0.0 copy-start.6
  52.3 0.0 copy-start.7
  52.3 14.3 %all-to-all-done.2.parts_ref = bf16[32,80,128]{2,1,0:T(8,128)(2,1)S(1)} async-done(((bf16[32,80,128]{2,1,0:T(8,128)(2,1)}), bf16[32,80,128]{2,1,0:T(8,128)(2,1)S(1)}, u32[]{:S(2)}, u32[]{:S(2)}) %all-to-all-start.2) | async-done | bytes 655392 | tf_op jit(solution)/shard_map/all_to_all | solution.py:422
  66.6 1.3 %shard_map.177 = (bf16[32,48,128]{2,1,0:T(8,128)(2,1)}, bf16[8,128]{1,0:T(8,128)(2,1)}) custom-call(bf16[32,80,128]{2,1,0:T(8,128)(2,1)S(1)} %all-to-all-done.2.parts_ref, bf16[128,2048]{1,0:T(8,128)(2,1)S(1)} %pad_maximum_fusion.weight_ref, bf16[8,128]{1,0:T(8,128)(2,1)S(1)} %pad_maximum_fusion.1.residual_ref, f32[8,128]{1,0:T(8,128)S(1)} %broadcast_in_dim.16.side_ref, ...), custom_call_target="tpu_custom_call" | custom-call | tf_op jit(solution)/shard_map/pallas_call | solution.py:437
  67.9 0.0 copy-start.1
  67.9 7.7 %all-to-all-start.3 = ((bf16[32,48,128]{2,1,0:T(8,128)(2,1)}), bf16[32,48,128]{2,1,0:T(8,128)(2,1)S(1)}, u32[]{:S(2)}, u32[]{:S(2)}) async-start(bf16[32,48,128]{2,1,0:T(8,128)(2,1)} %get-tuple-element.13), calls=%async_computation.3 | async-start | bytes 786432 | tf_op jit(solution)/shard_map/all_to_all | solution.py:451
  75.7 0.0 copy-done.5
  75.7 0.0 copy-done.6
  75.8 0.0 copy-done.7
  75.8 0.1 select_reduce_fusion
  75.9 10.1 %all-to-all-done.3.parts_ref = bf16[32,48,128]{2,1,0:T(8,128)(2,1)S(1)} async-done(((bf16[32,48,128]{2,1,0:T(8,128)(2,1)}), bf16[32,48,128]{2,1,0:T(8,128)(2,1)S(1)}, u32[]{:S(2)}, u32[]{:S(2)}) %all-to-all-start.3) | async-done | bytes 393248 | tf_op jit(solution)/shard_map/all_to_all | solution.py:451
  85.9 0.8 shard_map.179
  86.8 10.4 %all-to-all-start.4 = ((bf16[8,8,2048]{2,1,0:T(8,128)(2,1)}), bf16[8,8,2048]{2,1,0:T(8,128)(2,1)S(1)}, u32[]{:S(2)}, u32[]{:S(2)}) async-start(bf16[8,8,2048]{2,1,0:T(8,128)(2,1)} %get-tuple-element.16), calls=%async_computation.4 | async-start | bytes 524288 | tf_op jit(solution)/shard_map/all_to_all | solution.py:463
  97.2 0.1 copy.42.low_ref
  97.3 0.1 copy.43.high_ref
  97.4 0.1 compare_reduce_fusion
  97.5 6.2 %all-to-all-done.4.rows_ref = bf16[8,8,2048]{2,1,0:T(8,128)(2,1)S(1)} async-done(((bf16[8,8,2048]{2,1,0:T(8,128)(2,1)}), bf16[8,8,2048]{2,1,0:T(8,128)(2,1)S(1)}, u32[]{:S(2)}, u32[]{:S(2)}) %all-to-all-start.4) | async-done | bytes 262176 | tf_op jit(solution)/shard_map/all_to_all | solution.py:463
  103.7 0.0 copy-done.1
  103.7 1.4 %shard_map.180 = f32[32,8,128]{2,1,0:T(8,128)} custom-call(bf16[8,8,2048]{2,1,0:T(8,128)(2,1)S(1)} %all-to-all-done.4.rows_ref, bf16[400,2048]{1,0:T(8,128)(2,1)S(1)} %bitcast.36, s32[64,1]{1,0:T(8,128)S(1)} %copy.42.low_ref, s32[64,1]{1,0:T(8,128)S(1)} %copy.43.high_ref), custom_call_target="tpu_custom_call" | custom-call | tf_op jit(solution)/shard_map/pallas_call | solution.py:472
  105.1 6.3 %all-to-all-start.5 = ((f32[256,1,128]{2,1,0:T(1,128)}), f32[256,1,128]{2,1,0:T(1,128)S(1)}, u32[]{:S(2)}, u32[]{:S(2)}) async-start(f32[256,1,128]{2,1,0:T(1,128)} %bitcast.38), calls=%async_computation.5 | async-start | bytes 262144 | tf_op jit(solution)/shard_map/all_to_all | solution.py:475
  111.3 0.1 convolution_convert_fusion.1
  111.5 0.7 reshape.154
  112.2 1.1 shard_map.178
  113.3 0.6 slice_reduce_fusion
  113.9 10.3 %all-to-all-done.5 = f32[256,1,128]{2,1,0:T(1,128)S(1)} async-done(((f32[256,1,128]{2,1,0:T(1,128)}), f32[256,1,128]{2,1,0:T(1,128)S(1)}, u32[]{:S(2)}, u32[]{:S(2)}) %all-to-all-start.5) | async-done | bytes 131104 | tf_op jit(solution)/shard_map/all_to_all | solution.py:475
  124.2 0.8 reduce_max.9
  (15 shorter events, 0.1 us)
Async XLA Ops:
  0.6 22.9 %copy-start = (bf16[8,128,576]{1,2,0:T(8,128)(2,1)S(1)}, bf16[8,128,576]{1,2,0:T(8,128)(2,1)}, u32[]{:S(2)}) copy-start(bf16[8,128,576]{1,2,0:T(8,128)(2,1)} %param.19) | copy-start | bytes 3538948
  2.7 20.7 %all-to-all-start = ((bf16[32,8,128]{2,1,0:T(8,128)(2,1)}), bf16[32,8,128]{2,1,0:T(8,128)(2,1)S(1)}, u32[]{:S(2)}, u32[]{:S(2)}) async-start(bf16[32,8,128]{2,1,0:T(8,128)(2,1)} %shard_map.173), calls=%async_computation | async-start | bytes 131072 | tf_op jit(solution)/shard_map/all_to_all | solution.py:350
  23.5 10.3 %copy-start.4 = (s32[8,1,64]{2,1,0:T(1,128)S(1)}, s32[8,1,64]{2,1,0:T(1,128)}, u32[]{:S(2)}) copy-start(s32[8,1,64]{2,1,0:T(1,128)} %param.21) | copy-start | bytes 6148
  27.5 15.8 %all-to-all-start.1 = ((bf16[32,40,128]{2,1,0:T(8,128)(2,1)}), bf16[32,40,128]{2,1,0:T(8,128)(2,1)S(1)}, u32[]{:S(2)}, u32[]{:S(2)}) async-start(bf16[32,40,128]{2,1,0:T(8,128)(2,1)} %shard_map.174), calls=%async_computation.1 | async-start | bytes 655360 | tf_op jit(solution)/shard_map/all_to_all | solution.py:403
  43.4 7.8 %copy-start.3 = (s32[8,32]{1,0:T(8,128)S(1)}, s32[8,32]{1,0:T(8,128)}, u32[]{:S(2)}) copy-start(s32[8,32]{1,0:T(8,128)} %param.23) | copy-start | bytes 3076
  43.4 8.9 %copy-start.2 = (bf16[2048,64]{0,1:T(8,128)(2,1)S(1)}, bf16[2048,64]{0,1:T(8,128)(2,1)}, u32[]{:S(2)}) copy-start(bf16[2048,64]{0,1:T(8,128)(2,1)} %param.18) | copy-start | bytes 786436
  44.4 22.2 %all-to-all-start.2 = ((bf16[32,80,128]{2,1,0:T(8,128)(2,1)}), bf16[32,80,128]{2,1,0:T(8,128)(2,1)S(1)}, u32[]{:S(2)}, u32[]{:S(2)}) async-start(bf16[32,80,128]{2,1,0:T(8,128)(2,1)} %shard_map.176), calls=%async_computation.2 | async-start | bytes 1310720 | tf_op jit(solution)/shard_map/all_to_all | solution.py:422
  52.3 23.4 %copy-start.5 = (bf16[2048]{0:T(1024)(128)(2,1)S(1)}, bf16[2048]{0:T(1024)(128)(2,1)}, u32[]{:S(2)}) copy-start(bf16[2048]{0:T(1024)(128)(2,1)} %param.24) | copy-start | bytes 12292
  52.3 23.4 %copy-start.6 = (s32[4,2]{0,1:T(2,128)S(1)}, s32[4,2]{0,1:T(2,128)}, u32[]{:S(2)}) copy-start(s32[4,2]{0,1:T(2,128)} %param.26) | copy-start | bytes 100
  52.3 23.4 %copy-start.7 = (s32[64]{0:T(128)S(1)}, s32[64]{0:T(128)}, u32[]{:S(2)}) copy-start(s32[64]{0:T(128)} %param.27) | copy-start | bytes 772
  67.9 35.8 %copy-start.1 = (bf16[2048,400]{0,1:T(8,128)(2,1)S(1)}, bf16[2048,400]{0,1:T(8,128)(2,1)}, u32[]{:S(2)}) copy-start(bf16[2048,400]{0,1:T(8,128)(2,1)} %param.25) | copy-start | bytes 4915204
  67.9 18.0 %all-to-all-start.3 = ((bf16[32,48,128]{2,1,0:T(8,128)(2,1)}), bf16[32,48,128]{2,1,0:T(8,128)(2,1)S(1)}, u32[]{:S(2)}, u32[]{:S(2)}) async-start(bf16[32,48,128]{2,1,0:T(8,128)(2,1)} %get-tuple-element.13), calls=%async_computation.3 | async-start | bytes 786432 | tf_op jit(solution)/shard_map/all_to_all | solution.py:451
  86.8 16.9 %all-to-all-start.4 = ((bf16[8,8,2048]{2,1,0:T(8,128)(2,1)}), bf16[8,8,2048]{2,1,0:T(8,128)(2,1)S(1)}, u32[]{:S(2)}, u32[]{:S(2)}) async-start(bf16[8,8,2048]{2,1,0:T(8,128)(2,1)} %get-tuple-element.16), calls=%async_computation.4 | async-start | bytes 524288 | tf_op jit(solution)/shard_map/all_to_all | solution.py:463
  105.1 19.1 %all-to-all-start.5 = ((f32[256,1,128]{2,1,0:T(1,128)}), f32[256,1,128]{2,1,0:T(1,128)S(1)}, u32[]{:S(2)}, u32[]{:S(2)}) async-start(f32[256,1,128]{2,1,0:T(1,128)} %bitcast.38), calls=%async_computation.5 | async-start | bytes 262144 | tf_op jit(solution)/shard_map/all_to_all | solution.py:475

commit v3 on v2

--- a/solution.py
+++ b/solution.py
@@ -109,6 +109,10 @@
     fetch.wait()
 
 
+def mask_kernel(kept_ref, live_ref, absorb_ref, out_ref):
+    out_ref[...] = kept_ref[...] * live_ref[...]
+
+
 def attend_kernel(
     query_ref,
     absorb_ref,
@@ -121,24 +125,12 @@
     out_ref,
     lat_ref,
     tail_ref,
-    absorb_here,
-    sems,
 ):
-    parts = sems.shape[0]
-    step = H // parts
-    copies = []
-    for k in range(parts):
-        cut = slice(step * k, step * k + step)
-        copies.append(pltpu.make_async_copy(absorb_ref.at[cut], absorb_here.at[cut], sems.at[k]))
-    for copy in copies:
-        copy.start()
     for h in range(H):
-        if h % step == 0:
-            copies[h // step].wait()
         first = query_ref[2 * h].astype(F32)
         second = query_ref[2 * h + 1].astype(F32)
         nope = jnp.where(iota(first.shape, 1) < HALF, first, second).astype(BF16)
-        lat_ref[8 * h : 8 * h + 8, :] = mm(nope, absorb_here[h])
+        lat_ref[8 * h : 8 * h + 8, :] = mm(nope, absorb_ref[h])
         tail_ref[8 * h : 8 * h + 8, :] = second[:, :ROPE]
     lat = lat_ref[...].astype(BF16)
     tail = tail_ref[...].astype(BF16)
@@ -379,20 +371,19 @@
     )
 
     live_f = jnp.broadcast_to(live_here.astype(F32)[:, None], (RQ, BLK))
-    mask_f = live_f * kept_flag.astype(F32)
+    mask_f = vmem_call(mask_kernel, jax.ShapeDtypeStruct((RQ, BLK), F32))(
+        kept_flag.astype(F32), live_f, key_absorb
+    )
     part = vmem_call(
         attend_kernel,
         pltpu.HBM((seq_count, 40, 128), BF16),
         [
             pltpu.VMEM((H * RQ, LAT), F32),
             pltpu.VMEM((H * RQ, ROPE), F32),
-            pltpu.VMEM(key_absorb.shape, BF16),
-            pltpu.SemaphoreType.DMA((4,)),
         ],
-        in_specs=[WHOLE, APART] + [WHOLE] * 6,
     )(
         query_all,
-        pltpu.with_memory_space_constraint(key_absorb, pltpu.HBM),
+        key_absorb,
         cache_t,
         summary[:, :LAT],
         summary[:, LAT:],

time: 126 us -> 125 us (level)
  Pallas kernels: 14.1 us -> 12.8 us
    pallas_call x1, Pallas kernels: 3.99 us -> 2.56 us  [body(): vmem_call(attend_kernel, pltpu.HBM((seq_count, 40, 128), BF16), [pltpu.VM...]
  transfers between devices with their start and end apart: 6 -> 6, of which waited for: 6 -> 6; matrix products, arithmetic and copies ran while one was open for 8% -> 7% of each run, Pallas kernels for 3% -> 3%
where the time goes in v3:
time: 125 us; the launch traced here: 124 us
  waiting for transfers between devices  51.1 us (41%)
  starting transfers between devices  49.2 us (39%)
  Pallas kernels  12.8 us (10%)
  local copies, waits for them, and re-layouts  4.39 us (4%)
  other arithmetic  3.51 us (3%)
  matrix products  1.98 us (2%)
    all_to_all x1, waiting for transfers between devices, body(): values = lax.all_to_all(message, SEQ, 0, 0, tiled=True)  14.3 us
    all_to_all x1, starting transfers between devices, body(): query_all = lax.all_to_all(query_send, SEQ, 0, 0, tiled=True)  11.9 us
    all_to_all x1, starting transfers between devices, body(): normed = lax.all_to_all(normed, MP, 0, 0, tiled=True)  10.4 us
    all_to_all x1, waiting for transfers between devices, body(): lax.all_to_all(best.reshape(seq_count * mp_count, 1, 128), ALL, 0, 0, til...  10.3 us
    all_to_all x1, waiting for transfers between devices, body(): hidden_all = lax.all_to_all(hidden_send, SEQ, 0, 0, tiled=True)  10.1 us
    all_to_all x1, starting transfers between devices, body(): hidden_all = lax.all_to_all(hidden_send, SEQ, 0, 0, tiled=True)  7.74 us
    all_to_all x1, starting transfers between devices, body(): values = lax.all_to_all(message, SEQ, 0, 0, tiled=True)  6.79 us
    all_to_all x1, starting transfers between devices, body(): lax.all_to_all(best.reshape(seq_count * mp_count, 1, 128), ALL, 0, 0, til...  6.28 us
  transfers between devices with their start and end apart: 6, of which 6 were waited for; matrix products, arithmetic and copies ran while one was open for 7% of the time, Pallas kernels for 3%

profile of v3, /device:TPU:1, one launch (start us, length us, event | category | flops | bytes accessed | tf_op | source)
XLA Modules:
  0.0 123.9 jit_solution(7114692286940125861)
XLA Ops:
  0.6 0.0 copy-start.9
  0.6 0.0 copy-start.1
  0.7 2.1 %shard_map.173 = bf16[32,8,128]{2,1,0:T(8,128)(2,1)} custom-call(s32[1]{0:T(128)} %bitcast.side_ref, bf16[8,2048]{1,0:T(8,128)(2,1)} %hidden_ref.1, bf16[96,2048]{1,0:T(8,128)(2,1)} %bitcast.39), custom_call_target="tpu_custom_call" | custom-call | tf_op jit(solution)/shard_map/pallas_call | solution.py:328
  2.8 11.9 %all-to-all-start = ((bf16[32,8,128]{2,1,0:T(8,128)(2,1)}), bf16[32,8,128]{2,1,0:T(8,128)(2,1)S(1)}, u32[]{:S(2)}, u32[]{:S(2)}) async-start(bf16[32,8,128]{2,1,0:T(8,128)(2,1)} %shard_map.173), calls=%async_computation | async-start | bytes 131072 | tf_op jit(solution)/shard_map/all_to_all | solution.py:342
  14.7 0.9 dynamic-slice_reduce_fusion
  15.6 0.8 convert_reduce_fusion
  16.4 0.8 convert_reduce_fusion.1
  17.2 1.7 %fusion.6 = f32[8,1,576]{2,1,0:T(1,128)S(1)} fusion(bf16[8,128,576]{1,2,0:T(8,128)(2,1)} %param.19, bf16[8,128,1]{1,0,2:T(8,128)(2,1)S(1)} %bitcast.42), kind=kOutput, calls=%fused_computation.13 | convolution fusion | flops 1179648 | bytes 1200128 | tf_op jit(solution)/shard_map/nt,ntc->nc/dot_general | solution.py:350
  18.9 0.1 fusion.1
  19.0 0.1 convolution_convert_fusion
  19.2 0.0 copy-start
  19.2 0.1 reshape.151
  19.3 0.0 copy-done.9
  19.3 0.1 broadcast_in_dim.13.live_ref
  19.4 0.0 copy-done.1
  19.4 4.1 %all-to-all-done.query_ref = bf16[32,8,128]{2,1,0:T(8,128)(2,1)S(1)} async-done(((bf16[32,8,128]{2,1,0:T(8,128)(2,1)}), bf16[32,8,128]{2,1,0:T(8,128)(2,1)S(1)}, u32[]{:S(2)}, u32[]{:S(2)}) %all-to-all-start) | async-done | bytes 65568 | tf_op jit(solution)/shard_map/all_to_all | solution.py:342
  23.5 0.0 copy-done
  23.5 0.0 copy-start.5
  23.5 2.6 %shard_map.175 = bf16[32,40,128]{2,1,0:T(8,128)(2,1)} custom-call(bf16[32,8,128]{2,1,0:T(8,128)(2,1)S(1)} %all-to-all-done.query_ref, bf16[16,128,512]{2,1,0:T(8,128)(2,1)S(1)} %copy-done.1, bf16[8,576,128]{2,1,0:T(8,128)(2,1)S(1)} %bitcast.34, bf16[8,512]{1,0:T(8,128)(2,1)S(1)} %slice.32.summ_ref, bf16[8,64]{1,0:T(8,128)(2,1)S(1)} %slice.33.summ_tail_ref, ...), custom_call_target="tpu_custom_call" | custom-call | tf_op jit(solution)/shard_map/pallas_call | solution.py:377
  26.1 6.1 %all-to-all-start.1 = ((bf16[32,40,128]{2,1,0:T(8,128)(2,1)}), bf16[32,40,128]{2,1,0:T(8,128)(2,1)S(1)}, u32[]{:S(2)}, u32[]{:S(2)}) async-start(bf16[32,40,128]{2,1,0:T(8,128)(2,1)} %shard_map.175), calls=%async_computation.1 | async-start | bytes 655360 | tf_op jit(solution)/shard_map/all_to_all | solution.py:394
  32.2 0.5 broadcast.173
  32.7 0.0 copy-done.5
  32.7 0.7 reduce.8
  33.4 0.1 reshape_squeeze.3
  33.5 0.1 copy.38
  33.6 2.4 %shard_map.176 = (bf16[32,80,128]{2,1,0:T(8,128)(2,1)}, bf16[512,128]{1,0:T(8,128)(2,1)S(1)}) custom-call(s32[1]{0:T(128)} %bitcast.6.head_ref, bf16[8,576,128]{2,1,0:T(8,128)(2,1)S(1)} %bitcast.35, s32[256,2]{1,0:T(8,128)S(1)} %bitcast.37, bf16[16,512,128]{2,1,0:T(8,128)(2,1)} %up_ref.1), custom_call_target="tpu_custom_call" | custom-call | tf_op jit(solution)/shard_map/pallas_call | solution.py:360
  36.1 6.2 %all-to-all-done.1.parts_ref = bf16[32,40,128]{2,1,0:T(8,128)(2,1)S(1)} async-done(((bf16[32,40,128]{2,1,0:T(8,128)(2,1)}), bf16[32,40,128]{2,1,0:T(8,128)(2,1)S(1)}, u32[]{:S(2)}, u32[]{:S(2)}) %all-to-all-start.1) | async-done | bytes 327712 | tf_op jit(solution)/shard_map/all_to_all | solution.py:394
  42.2 0.1 broadcast_in_dim.15.half_ref
  42.3 0.0 copy-start.4
  42.3 0.0 copy-start.3
  42.3 1.0 shard_map.177
  43.3 6.8 %all-to-all-start.2 = ((bf16[32,80,128]{2,1,0:T(8,128)(2,1)}), bf16[32,80,128]{2,1,0:T(8,128)(2,1)S(1)}, u32[]{:S(2)}, u32[]{:S(2)}) async-start(bf16[32,80,128]{2,1,0:T(8,128)(2,1)} %shard_map.177), calls=%async_computation.2 | async-start | bytes 1310720 | tf_op jit(solution)/shard_map/all_to_all | solution.py:413
  50.1 0.0 copy-done.4
  50.1 0.1 copy.39
  50.2 0.1 reshape.153.dest_ref
  50.3 0.8 constant_dynamic-slice_fusion
  51.1 0.1 pad_maximum_fusion.1.residual_ref
  51.2 0.0 copy-done.3
  51.2 0.0 copy-start.6
  51.2 0.0 copy-start.7
  51.2 0.0 copy-start.8
  51.3 14.3 %all-to-all-done.2.parts_ref = bf16[32,80,128]{2,1,0:T(8,128)(2,1)S(1)} async-done(((bf16[32,80,128]{2,1,0:T(8,128)(2,1)}), bf16[32,80,128]{2,1,0:T(8,128)(2,1)S(1)}, u32[]{:S(2)}, u32[]{:S(2)}) %all-to-all-start.2) | async-done | bytes 655392 | tf_op jit(solution)/shard_map/all_to_all | solution.py:413
  65.6 1.3 %shard_map.178 = (bf16[32,48,128]{2,1,0:T(8,128)(2,1)}, bf16[8,128]{1,0:T(8,128)(2,1)}) custom-call(bf16[32,80,128]{2,1,0:T(8,128)(2,1)S(1)} %all-to-all-done.2.parts_ref, bf16[128,2048]{1,0:T(8,128)(2,1)S(1)} %pad_maximum_fusion.weight_ref, bf16[8,128]{1,0:T(8,128)(2,1)S(1)} %pad_maximum_fusion.1.residual_ref, f32[8,128]{1,0:T(8,128)S(1)} %broadcast_in_dim.16.side_ref, ...), custom_call_target="tpu_custom_call" | custom-call | tf_op jit(solution)/shard_map/pallas_call | solution.py:428
  66.9 7.7 %all-to-all-start.3 = ((bf16[32,48,128]{2,1,0:T(8,128)(2,1)}), bf16[32,48,128]{2,1,0:T(8,128)(2,1)S(1)}, u32[]{:S(2)}, u32[]{:S(2)}) async-start(bf16[32,48,128]{2,1,0:T(8,128)(2,1)} %get-tuple-element.13), calls=%async_computation.3 | async-start | bytes 786432 | tf_op jit(solution)/shard_map/all_to_all | solution.py:442
  74.7 0.0 copy-done.6
  74.7 0.0 copy-done.7
  74.7 0.0 copy-done.8
  74.7 0.1 select_reduce_fusion
  74.8 10.1 %all-to-all-done.3.parts_ref = bf16[32,48,128]{2,1,0:T(8,128)(2,1)S(1)} async-done(((bf16[32,48,128]{2,1,0:T(8,128)(2,1)}), bf16[32,48,128]{2,1,0:T(8,128)(2,1)S(1)}, u32[]{:S(2)}, u32[]{:S(2)}) %all-to-all-start.3) | async-done | bytes 393248 | tf_op jit(solution)/shard_map/all_to_all | solution.py:442
  84.9 0.8 shard_map.180
  85.7 10.4 %all-to-all-start.4 = ((bf16[8,8,2048]{2,1,0:T(8,128)(2,1)}), bf16[8,8,2048]{2,1,0:T(8,128)(2,1)S(1)}, u32[]{:S(2)}, u32[]{:S(2)}) async-start(bf16[8,8,2048]{2,1,0:T(8,128)(2,1)} %get-tuple-element.16), calls=%async_computation.4 | async-start | bytes 524288 | tf_op jit(solution)/shard_map/all_to_all | solution.py:454
  96.2 0.1 copy.42.low_ref
  96.3 0.1 copy.43.high_ref
  96.4 0.1 compare_reduce_fusion
  96.5 6.2 %all-to-all-done.4.rows_ref = bf16[8,8,2048]{2,1,0:T(8,128)(2,1)S(1)} async-done(((bf16[8,8,2048]{2,1,0:T(8,128)(2,1)}), bf16[8,8,2048]{2,1,0:T(8,128)(2,1)S(1)}, u32[]{:S(2)}, u32[]{:S(2)}) %all-to-all-start.4) | async-done | bytes 262176 | tf_op jit(solution)/shard_map/all_to_all | solution.py:454
  102.7 0.0 copy-done.2
  102.7 1.4 %shard_map.181 = f32[32,8,128]{2,1,0:T(8,128)} custom-call(bf16[8,8,2048]{2,1,0:T(8,128)(2,1)S(1)} %all-to-all-done.4.rows_ref, bf16[400,2048]{1,0:T(8,128)(2,1)S(1)} %bitcast.36, s32[64,1]{1,0:T(8,128)S(1)} %copy.42.low_ref, s32[64,1]{1,0:T(8,128)S(1)} %copy.43.high_ref), custom_call_target="tpu_custom_call" | custom-call | tf_op jit(solution)/shard_map/pallas_call | solution.py:463
  104.0 6.3 %all-to-all-start.5 = ((f32[256,1,128]{2,1,0:T(1,128)}), f32[256,1,128]{2,1,0:T(1,128)S(1)}, u32[]{:S(2)}, u32[]{:S(2)}) async-start(f32[256,1,128]{2,1,0:T(1,128)} %bitcast.38), calls=%async_computation.5 | async-start | bytes 262144 | tf_op jit(solution)/shard_map/all_to_all | solution.py:466
  110.3 0.1 convolution_convert_fusion.1
  110.4 0.7 reshape.154
  111.1 1.1 shard_map.179
  112.2 0.6 slice_reduce_fusion
  112.9 10.3 %all-to-all-done.5 = f32[256,1,128]{2,1,0:T(1,128)S(1)} async-done(((f32[256,1,128]{2,1,0:T(1,128)}), f32[256,1,128]{2,1,0:T(1,128)S(1)}, u32[]{:S(2)}, u32[]{:S(2)}) %all-to-all-start.5) | async-done | bytes 131104 | tf_op jit(solution)/shard_map/all_to_all | solution.py:466
  123.1 0.8 reduce_max.9
  (19 shorter events, 0.1 us)
Async XLA Ops:
  0.6 18.7 %copy-start.9 = (s32[8]{0:T(128)S(1)}, s32[8]{0:T(128)}, u32[]{:S(2)}) copy-start(s32[8]{0:T(128)} %param.20) | copy-start | bytes 100
  0.6 18.8 %copy-start.1 = (bf16[16,128,512]{2,1,0:T(8,128)(2,1)S(1)}, bf16[16,128,512]{2,1,0:T(8,128)(2,1)}, u32[]{:S(2)}) copy-start(bf16[16,128,512]{2,1,0:T(8,128)(2,1)} %absorb_ref.3) | copy-start | bytes 6291460
  2.8 20.7 %all-to-all-start = ((bf16[32,8,128]{2,1,0:T(8,128)(2,1)}), bf16[32,8,128]{2,1,0:T(8,128)(2,1)S(1)}, u32[]{:S(2)}, u32[]{:S(2)}) async-start(bf16[32,8,128]{2,1,0:T(8,128)(2,1)} %shard_map.173), calls=%async_computation | async-start | bytes 131072 | tf_op jit(solution)/shard_map/all_to_all | solution.py:342
  19.2 4.4 %copy-start = (bf16[8,128,576]{1,2,0:T(8,128)(2,1)S(1)}, bf16[8,128,576]{1,2,0:T(8,128)(2,1)}, u32[]{:S(2)}) copy-start(bf16[8,128,576]{1,2,0:T(8,128)(2,1)} %param.19) | copy-start | bytes 3538948
  23.5 9.2 %copy-start.5 = (s32[8,1,64]{2,1,0:T(1,128)S(1)}, s32[8,1,64]{2,1,0:T(1,128)}, u32[]{:S(2)}) copy-start(s32[8,1,64]{2,1,0:T(1,128)} %param.21) | copy-start | bytes 6148
  26.1 16.1 %all-to-all-start.1 = ((bf16[32,40,128]{2,1,0:T(8,128)(2,1)}), bf16[32,40,128]{2,1,0:T(8,128)(2,1)S(1)}, u32[]{:S(2)}, u32[]{:S(2)}) async-start(bf16[32,40,128]{2,1,0:T(8,128)(2,1)} %shard_map.175), calls=%async_computation.1 | async-start | bytes 655360 | tf_op jit(solution)/shard_map/all_to_all | solution.py:394
  42.3 7.8 %copy-start.4 = (s32[8,32]{1,0:T(8,128)S(1)}, s32[8,32]{1,0:T(8,128)}, u32[]{:S(2)}) copy-start(s32[8,32]{1,0:T(8,128)} %param.23) | copy-start | bytes 3076
  42.3 8.9 %copy-start.3 = (bf16[2048,64]{0,1:T(8,128)(2,1)S(1)}, bf16[2048,64]{0,1:T(8,128)(2,1)}, u32[]{:S(2)}) copy-start(bf16[2048,64]{0,1:T(8,128)(2,1)} %param.18) | copy-start | bytes 786436
  43.3 22.2 %all-to-all-start.2 = ((bf16[32,80,128]{2,1,0:T(8,128)(2,1)}), bf16[32,80,128]{2,1,0:T(8,128)(2,1)S(1)}, u32[]{:S(2)}, u32[]{:S(2)}) async-start(bf16[32,80,128]{2,1,0:T(8,128)(2,1)} %shard_map.177), calls=%async_computation.2 | async-start | bytes 1310720 | tf_op jit(solution)/shard_map/all_to_all | solution.py:413
  51.2 23.4 %copy-start.6 = (bf16[2048]{0:T(1024)(128)(2,1)S(1)}, bf16[2048]{0:T(1024)(128)(2,1)}, u32[]{:S(2)}) copy-start(bf16[2048]{0:T(1024)(128)(2,1)} %param.24) | copy-start | bytes 12292
  51.2 23.5 %copy-start.7 = (s32[4,2]{0,1:T(2,128)S(1)}, s32[4,2]{0,1:T(2,128)}, u32[]{:S(2)}) copy-start(s32[4,2]{0,1:T(2,128)} %param.26) | copy-start | bytes 100
  51.2 23.5 %copy-start.8 = (s32[64]{0:T(128)S(1)}, s32[64]{0:T(128)}, u32[]{:S(2)}) copy-start(s32[64]{0:T(128)} %param.27) | copy-start | bytes 772
  66.9 35.8 %copy-start.2 = (bf16[2048,400]{0,1:T(8,128)(2,1)S(1)}, bf16[2048,400]{0,1:T(8,128)(2,1)}, u32[]{:S(2)}) copy-start(bf16[2048,400]{0,1:T(8,128)(2,1)} %param.25) | copy-start | bytes 4915204
  66.9 18.0 %all-to-all-start.3 = ((bf16[32,48,128]{2,1,0:T(8,128)(2,1)}), bf16[32,48,128]{2,1,0:T(8,128)(2,1)S(1)}, u32[]{:S(2)}, u32[]{:S(2)}) async-start(bf16[32,48,128]{2,1,0:T(8,128)(2,1)} %get-tuple-element.13), calls=%async_computation.3 | async-start | bytes 786432 | tf_op jit(solution)/shard_map/all_to_all | solution.py:442
  85.7 16.9 %all-to-all-start.4 = ((bf16[8,8,2048]{2,1,0:T(8,128)(2,1)}), bf16[8,8,2048]{2,1,0:T(8,128)(2,1)S(1)}, u32[]{:S(2)}, u32[]{:S(2)}) async-start(bf16[8,8,2048]{2,1,0:T(8,128)(2,1)} %get-tuple-element.16), calls=%async_computation.4 | async-start | bytes 524288 | tf_op jit(solution)/shard_map/all_to_all | solution.py:454
  104.0 19.1 %all-to-all-start.5 = ((f32[256,1,128]{2,1,0:T(1,128)}), f32[256,1,128]{2,1,0:T(1,128)S(1)}, u32[]{:S(2)}, u32[]{:S(2)}) async-start(f32[256,1,128]{2,1,0:T(1,128)} %bitcast.38), calls=%async_computation.5 | async-start | bytes 262144 | tf_op jit(solution)/shard_map/all_to_all | solution.py:466

commit v4 on v3

--- a/solution.py
+++ b/solution.py
@@ -19,7 +19,8 @@
 ROW = LAT + ROPE
 HALF = (NOPE + ROPE) // 2
 WIDE = H * VH
-SEQ = ("sx", "sz")
+SEQ = ("sx", "z1", "z0")
+TURN = ("z0", "sx", "z1")
 MP = ("y", "c")
 ALL = SEQ + MP
 
@@ -44,6 +45,11 @@
 WHOLE = pl.BlockSpec(memory_space=pltpu.VMEM)
 APART = pl.BlockSpec(memory_space=pltpu.HBM)
 SCALAR = pl.BlockSpec(memory_space=pltpu.SMEM)
+
+
+def turned(x, sizes):
+    x = x.reshape(sizes + x.shape[1:])
+    return jnp.moveaxis(x, 2, 0).reshape((-1,) + x.shape[3:])
 
 
 def vmem_call(kernel, out_shape, scratch=(), limit=16 << 20, **specs):
@@ -219,10 +225,13 @@
     copy.wait()
 
 
-def hidden_kernel(parts_ref, weight_ref, residual_ref, side_ref, dest_ref, out_ref, own_ref):
+def hidden_kernel(rank_of, parts_ref, weight_ref, residual_ref, side_ref, dest_ref, out_ref, own_ref):
     count = parts_ref.shape[0]
     values = [
-        (parts_ref[2 * h, :RQ, :].astype(F32) + parts_ref[2 * h + 1, :RQ, :].astype(F32)).astype(BF16)
+        (
+            parts_ref[rank_of[2 * h], :RQ, :].astype(F32)
+            + parts_ref[rank_of[2 * h + 1], :RQ, :].astype(F32)
+        ).astype(BF16)
         for h in range(H)
     ]
     total = mm_nt(jnp.concatenate(values, axis=1), weight_ref[...])
@@ -248,13 +257,14 @@
         out_ref[:, RQ + RQ * q : 2 * RQ + RQ * q, :] = picked.astype(BF16).reshape(count, RQ, 128)
 
 
-def settle_kernel(parts_ref, out_ref):
+def settle_kernel(inner, parts_ref, out_ref):
     count = parts_ref.shape[0]
     rows = count * RQ
     row = iota((rows, rows), 0)
     column = iota((rows, rows), 1)
     slot, keep = row // KB, row % KB
-    from_row = keep % count * RQ + slot
+    rank = keep % count
+    from_row = (rank % (count // inner) * inner + rank // (count // inner)) * RQ + slot
     whole = (column == from_row + keep // count * (RQ // 2)).astype(F32).astype(BF16)
     tail = (column == from_row).astype(F32).astype(BF16)
 
@@ -319,7 +329,9 @@
     tenant_ranges,
     tenant_ids,
 ):
-    seq_count = lax.axis_size("sx") * lax.axis_size("sz")
+    sizes = (lax.axis_size("sx"), lax.axis_size("z1"), lax.axis_size("z0"))
+    seq_count = sizes[0] * sizes[1] * sizes[2]
+    rank_of = [s % sizes[2] * (seq_count // sizes[2]) + s // sizes[2] for s in range(seq_count)]
     mp_count = lax.axis_size("y") * lax.axis_size("c")
     seq_index = lax.axis_index(SEQ)
     mp_index = lax.axis_index(MP)
@@ -410,7 +422,7 @@
         jnp.broadcast_to(half[:, None], (RQ, 128)),
         message,
     )
-    values = lax.all_to_all(message, SEQ, 0, 0, tiled=True)
+    values = lax.all_to_all(message, TURN, 0, 0, tiled=True)
     slots = seq_index * slot_count + jnp.arange(slot_count, dtype=jnp.int32)
     summ_pick = jnp.any(pack_dest[None, :, :] == slots[:, None, None], axis=1)
     packed_summary = jnp.einsum(
@@ -426,7 +438,7 @@
     out_t = out_weight.T
     side = (jnp.arange(2 * col_width) // col_width == seq_index % 2).astype(F32)
     hidden_send, own = vmem_call(
-        hidden_kernel,
+        functools.partial(hidden_kernel, rank_of),
         (
             pltpu.HBM((seq_count, 48, 128), BF16),
             jax.ShapeDtypeStruct((RQ, 2 * col_width), BF16),
@@ -436,11 +448,11 @@
         jnp.concatenate([out_t, out_t], axis=0),
         jnp.concatenate([residual, residual], axis=1),
         jnp.broadcast_to(side[None, :], (RQ, 2 * col_width)),
-        pack_dest.T.reshape(1, -1),
+        turned(pack_dest.T, sizes).reshape(1, -1),
     )
     hidden_out = own[:, :col_width]
     hidden_all = lax.all_to_all(hidden_send, SEQ, 0, 0, tiled=True)
-    packed_rows = vmem_call(settle_kernel, jax.ShapeDtypeStruct((slot_count, KB, ROW), BF16))(
+    packed_rows = vmem_call(functools.partial(settle_kernel, sizes[2]), jax.ShapeDtypeStruct((slot_count, KB, ROW), BF16))(
         hidden_all
     )
     normed, norms = vmem_call(
@@ -471,7 +483,7 @@
 def solution(mesh):
     seq_count, mp_count = mesh.devices.shape
     split = Mesh(
-        mesh.devices.reshape(4, seq_count // 4, mp_count // 2, 2), ("sx", "sz", "y", "c")
+        mesh.devices.reshape(4, 2, seq_count // 8, mp_count // 2, 2), SEQ + MP
     )
     in_specs = (
         P(MP, None),

time: 125 us -> 125 us (level)
  no operation moved by 1% of the time
where the time goes in v4:
time: 125 us; the launch traced here: 124 us
  waiting for transfers between devices  51.6 us (41%)
  starting transfers between devices  49.1 us (39%)
  Pallas kernels  12.7 us (10%)
  local copies, waits for them, and re-layouts  4.4 us (4%)
  other arithmetic  3.51 us (3%)
  matrix products  1.98 us (2%)
    all_to_all x1, waiting for transfers between devices, body(): values = lax.all_to_all(message, TURN, 0, 0, tiled=True)  14.8 us
    all_to_all x1, starting transfers between devices, body(): query_all = lax.all_to_all(query_send, SEQ, 0, 0, tiled=True)  11.9 us
    all_to_all x1, waiting for transfers between devices, body(): lax.all_to_all(best.reshape(seq_count * mp_count, 1, 128), ALL, 0, 0, til...  10.3 us
    all_to_all x1, waiting for transfers between devices, body(): hidden_all = lax.all_to_all(hidden_send, SEQ, 0, 0, tiled=True)  10.1 us
    all_to_all x1, starting transfers between devices, body(): normed = lax.all_to_all(normed, MP, 0, 0, tiled=True)  9.73 us
    all_to_all x1, starting transfers between devices, body(): hidden_all = lax.all_to_all(hidden_send, SEQ, 0, 0, tiled=True)  7.65 us
    all_to_all x1, starting transfers between devices, body(): lax.all_to_all(best.reshape(seq_count * mp_count, 1, 128), ALL, 0, 0, til...  6.96 us
    all_to_all x1, starting transfers between devices, body(): values = lax.all_to_all(message, TURN, 0, 0, tiled=True)  6.78 us
  transfers between devices with their start and end apart: 6, of which 6 were waited for; matrix products, arithmetic and copies ran while one was open for 7% of the time, Pallas kernels for 3%

profile of v4, /device:TPU:1, one launch (start us, length us, event | category | flops | bytes accessed | tf_op | source)
XLA Modules:
  0.0 124.3 jit_solution(7437219136793431694)
XLA Ops:
  0.6 0.0 copy-start.9
  0.6 0.0 copy-start.1
  0.7 2.1 %shard_map.173 = bf16[32,8,128]{2,1,0:T(8,128)(2,1)} custom-call(s32[1]{0:T(128)} %bitcast.side_ref, bf16[8,2048]{1,0:T(8,128)(2,1)} %hidden_ref.1, bf16[96,2048]{1,0:T(8,128)(2,1)} %bitcast.43), custom_call_target="tpu_custom_call" | custom-call | tf_op jit(solution)/shard_map/pallas_call | solution.py:340
  2.8 11.9 %all-to-all-start = ((bf16[32,8,128]{2,1,0:T(8,128)(2,1)}), bf16[32,8,128]{2,1,0:T(8,128)(2,1)S(1)}, u32[]{:S(2)}, u32[]{:S(2)}) async-start(bf16[32,8,128]{2,1,0:T(8,128)(2,1)} %shard_map.173), calls=%async_computation | async-start | bytes 131072 | tf_op jit(solution)/shard_map/all_to_all | solution.py:354
  14.7 0.9 dynamic-slice_reduce_fusion
  15.6 0.8 convert_reduce_fusion
  16.4 0.8 convert_reduce_fusion.1
  17.2 1.7 %fusion.6 = f32[8,1,576]{2,1,0:T(1,128)S(1)} fusion(bf16[8,128,576]{1,2,0:T(8,128)(2,1)} %param.19, bf16[8,128,1]{1,0,2:T(8,128)(2,1)S(1)} %bitcast.46), kind=kOutput, calls=%fused_computation.13 | convolution fusion | flops 1179648 | bytes 1200128 | tf_op jit(solution)/shard_map/nt,ntc->nc/dot_general | solution.py:362
  18.9 0.1 fusion.1
  19.0 0.1 convolution_convert_fusion
  19.2 0.0 copy-start
  19.2 0.1 reshape.151
  19.3 0.0 copy-done.9
  19.3 0.1 broadcast_in_dim.13.live_ref
  19.4 0.0 copy-done.1
  19.4 4.1 %all-to-all-done.query_ref = bf16[32,8,128]{2,1,0:T(8,128)(2,1)S(1)} async-done(((bf16[32,8,128]{2,1,0:T(8,128)(2,1)}), bf16[32,8,128]{2,1,0:T(8,128)(2,1)S(1)}, u32[]{:S(2)}, u32[]{:S(2)}) %all-to-all-start) | async-done | bytes 65568 | tf_op jit(solution)/shard_map/all_to_all | solution.py:354
  23.5 0.0 copy-done
  23.5 0.0 copy-start.5
  23.5 2.6 %shard_map.175 = bf16[32,40,128]{2,1,0:T(8,128)(2,1)} custom-call(bf16[32,8,128]{2,1,0:T(8,128)(2,1)S(1)} %all-to-all-done.query_ref, bf16[16,128,512]{2,1,0:T(8,128)(2,1)S(1)} %copy-done.1, bf16[8,576,128]{2,1,0:T(8,128)(2,1)S(1)} %bitcast.38, bf16[8,512]{1,0:T(8,128)(2,1)S(1)} %slice.32.summ_ref, bf16[8,64]{1,0:T(8,128)(2,1)S(1)} %slice.33.summ_tail_ref, ...), custom_call_target="tpu_custom_call" | custom-call | tf_op jit(solution)/shard_map/pallas_call | solution.py:389
  26.1 6.1 %all-to-all-start.1 = ((bf16[32,40,128]{2,1,0:T(8,128)(2,1)}), bf16[32,40,128]{2,1,0:T(8,128)(2,1)S(1)}, u32[]{:S(2)}, u32[]{:S(2)}) async-start(bf16[32,40,128]{2,1,0:T(8,128)(2,1)} %shard_map.175), calls=%async_computation.1 | async-start | bytes 655360 | tf_op jit(solution)/shard_map/all_to_all | solution.py:406
  32.2 0.5 broadcast.173
  32.7 0.0 copy-done.5
  32.7 0.7 reduce.8
  33.4 0.1 reshape_squeeze.3
  33.5 0.1 copy.40
  33.6 2.4 %shard_map.176 = (bf16[32,80,128]{2,1,0:T(8,128)(2,1)}, bf16[512,128]{1,0:T(8,128)(2,1)S(1)}) custom-call(s32[1]{0:T(128)} %bitcast.6.head_ref, bf16[8,576,128]{2,1,0:T(8,128)(2,1)S(1)} %bitcast.39, s32[256,2]{1,0:T(8,128)S(1)} %bitcast.41, bf16[16,512,128]{2,1,0:T(8,128)(2,1)} %up_ref.1), custom_call_target="tpu_custom_call" | custom-call | tf_op jit(solution)/shard_map/pallas_call | solution.py:372
  36.1 6.2 %all-to-all-done.1.parts_ref = bf16[32,40,128]{2,1,0:T(8,128)(2,1)S(1)} async-done(((bf16[32,40,128]{2,1,0:T(8,128)(2,1)}), bf16[32,40,128]{2,1,0:T(8,128)(2,1)S(1)}, u32[]{:S(2)}, u32[]{:S(2)}) %all-to-all-start.1) | async-done | bytes 327712 | tf_op jit(solution)/shard_map/all_to_all | solution.py:406
  42.2 0.1 broadcast_in_dim.15.half_ref
  42.3 0.0 copy-start.4
  42.3 0.0 copy-start.3
  42.3 1.0 shard_map.177
  43.3 6.8 %all-to-all-start.2 = ((bf16[32,80,128]{2,1,0:T(8,128)(2,1)}), bf16[32,80,128]{2,1,0:T(8,128)(2,1)S(1)}, u32[]{:S(2)}, u32[]{:S(2)}) async-start(bf16[32,80,128]{2,1,0:T(8,128)(2,1)} %shard_map.177), calls=%async_computation.2 | async-start | bytes 1310720 | tf_op jit(solution)/shard_map/all_to_all | solution.py:425
  50.1 0.0 copy-done.4
  50.1 0.1 copy.41
  50.2 0.1 reshape_reshape.3.dest_ref
  50.3 0.8 constant_dynamic-slice_fusion
  51.1 0.1 pad_maximum_fusion.1.residual_ref
  51.2 0.0 copy-done.3
  51.2 0.0 copy-start.6
  51.3 0.0 copy-start.7
  51.3 0.0 copy-start.8
  51.3 14.8 %all-to-all-done.2.parts_ref = bf16[32,80,128]{2,1,0:T(8,128)(2,1)S(1)} async-done(((bf16[32,80,128]{2,1,0:T(8,128)(2,1)}), bf16[32,80,128]{2,1,0:T(8,128)(2,1)S(1)}, u32[]{:S(2)}, u32[]{:S(2)}) %all-to-all-start.2) | async-done | bytes 655392 | tf_op jit(solution)/shard_map/all_to_all | solution.py:425
  66.1 1.3 %shard_map.178 = (bf16[32,48,128]{2,1,0:T(8,128)(2,1)}, bf16[8,128]{1,0:T(8,128)(2,1)}) custom-call(bf16[32,80,128]{2,1,0:T(8,128)(2,1)S(1)} %all-to-all-done.2.parts_ref, bf16[128,2048]{1,0:T(8,128)(2,1)S(1)} %pad_maximum_fusion.weight_ref, bf16[8,128]{1,0:T(8,128)(2,1)S(1)} %pad_maximum_fusion.1.residual_ref, f32[8,128]{1,0:T(8,128)S(1)} %broadcast_in_dim.16.side_ref, ...), custom_call_target="tpu_custom_call" | custom-call | tf_op jit(solution)/shard_map/pallas_call | solution.py:440
  67.4 7.7 %all-to-all-start.3 = ((bf16[32,48,128]{2,1,0:T(8,128)(2,1)}), bf16[32,48,128]{2,1,0:T(8,128)(2,1)S(1)}, u32[]{:S(2)}, u32[]{:S(2)}) async-start(bf16[32,48,128]{2,1,0:T(8,128)(2,1)} %get-tuple-element.13), calls=%async_computation.3 | async-start | bytes 786432 | tf_op jit(solution)/shard_map/all_to_all | solution.py:454
  75.1 0.0 copy-done.6
  75.1 0.0 copy-done.7
  75.1 0.0 copy-done.8
  75.1 0.1 select_reduce_fusion
  75.2 10.1 %all-to-all-done.3.parts_ref = bf16[32,48,128]{2,1,0:T(8,128)(2,1)S(1)} async-done(((bf16[32,48,128]{2,1,0:T(8,128)(2,1)}), bf16[32,48,128]{2,1,0:T(8,128)(2,1)S(1)}, u32[]{:S(2)}, u32[]{:S(2)}) %all-to-all-start.3) | async-done | bytes 393248 | tf_op jit(solution)/shard_map/all_to_all | solution.py:454
  85.3 0.8 shard_map.180
  86.1 9.7 %all-to-all-start.4 = ((bf16[8,8,2048]{2,1,0:T(8,128)(2,1)}), bf16[8,8,2048]{2,1,0:T(8,128)(2,1)S(1)}, u32[]{:S(2)}, u32[]{:S(2)}) async-start(bf16[8,8,2048]{2,1,0:T(8,128)(2,1)} %get-tuple-element.16), calls=%async_computation.4 | async-start | bytes 524288 | tf_op jit(solution)/shard_map/all_to_all | solution.py:466
  95.9 0.1 copy.45.low_ref
  96.0 0.1 copy.46.high_ref
  96.1 0.1 compare_reduce_fusion
  96.2 6.2 %all-to-all-done.4.rows_ref = bf16[8,8,2048]{2,1,0:T(8,128)(2,1)S(1)} async-done(((bf16[8,8,2048]{2,1,0:T(8,128)(2,1)}), bf16[8,8,2048]{2,1,0:T(8,128)(2,1)S(1)}, u32[]{:S(2)}, u32[]{:S(2)}) %all-to-all-start.4) | async-done | bytes 262176 | tf_op jit(solution)/shard_map/all_to_all | solution.py:466
  102.4 0.0 copy-done.2
  102.4 1.4 %shard_map.181 = f32[32,8,128]{2,1,0:T(8,128)} custom-call(bf16[8,8,2048]{2,1,0:T(8,128)(2,1)S(1)} %all-to-all-done.4.rows_ref, bf16[400,2048]{1,0:T(8,128)(2,1)S(1)} %bitcast.40, s32[64,1]{1,0:T(8,128)S(1)} %copy.45.low_ref, s32[64,1]{1,0:T(8,128)S(1)} %copy.46.high_ref), custom_call_target="tpu_custom_call" | custom-call | tf_op jit(solution)/shard_map/pallas_call | solution.py:475
  103.7 7.0 %all-to-all-start.5 = ((f32[256,1,128]{2,1,0:T(1,128)}), f32[256,1,128]{2,1,0:T(1,128)S(1)}, u32[]{:S(2)}, u32[]{:S(2)}) async-start(f32[256,1,128]{2,1,0:T(1,128)} %bitcast.42), calls=%async_computation.5 | async-start | bytes 262144 | tf_op jit(solution)/shard_map/all_to_all | solution.py:478
  110.7 0.1 convolution_convert_fusion.1
  110.8 0.7 reshape.154
  111.5 1.1 shard_map.179
  112.6 0.6 slice_reduce_fusion
  113.3 10.3 %all-to-all-done.5 = f32[256,1,128]{2,1,0:T(1,128)S(1)} async-done(((f32[256,1,128]{2,1,0:T(1,128)}), f32[256,1,128]{2,1,0:T(1,128)S(1)}, u32[]{:S(2)}, u32[]{:S(2)}) %all-to-all-start.5) | async-done | bytes 131104 | tf_op jit(solution)/shard_map/all_to_all | solution.py:478
  123.5 0.8 reduce_max.9
  (20 shorter events, 0.2 us)
Async XLA Ops:
  0.6 18.7 %copy-start.9 = (s32[8]{0:T(128)S(1)}, s32[8]{0:T(128)}, u32[]{:S(2)}) copy-start(s32[8]{0:T(128)} %param.20) | copy-start | bytes 100
  0.6 18.8 %copy-start.1 = (bf16[16,128,512]{2,1,0:T(8,128)(2,1)S(1)}, bf16[16,128,512]{2,1,0:T(8,128)(2,1)}, u32[]{:S(2)}) copy-start(bf16[16,128,512]{2,1,0:T(8,128)(2,1)} %absorb_ref.3) | copy-start | bytes 6291460
  2.8 20.7 %all-to-all-start = ((bf16[32,8,128]{2,1,0:T(8,128)(2,1)}), bf16[32,8,128]{2,1,0:T(8,128)(2,1)S(1)}, u32[]{:S(2)}, u32[]{:S(2)}) async-start(bf16[32,8,128]{2,1,0:T(8,128)(2,1)} %shard_map.173), calls=%async_computation | async-start | bytes 131072 | tf_op jit(solution)/shard_map/all_to_all | solution.py:354
  19.2 4.4 %copy-start = (bf16[8,128,576]{1,2,0:T(8,128)(2,1)S(1)}, bf16[8,128,576]{1,2,0:T(8,128)(2,1)}, u32[]{:S(2)}) copy-start(bf16[8,128,576]{1,2,0:T(8,128)(2,1)} %param.19) | copy-start | bytes 3538948
  23.5 9.2 %copy-start.5 = (s32[8,1,64]{2,1,0:T(1,128)S(1)}, s32[8,1,64]{2,1,0:T(1,128)}, u32[]{:S(2)}) copy-start(s32[8,1,64]{2,1,0:T(1,128)} %param.21) | copy-start | bytes 6148
  26.1 16.2 %all-to-all-start.1 = ((bf16[32,40,128]{2,1,0:T(8,128)(2,1)}), bf16[32,40,128]{2,1,0:T(8,128)(2,1)S(1)}, u32[]{:S(2)}, u32[]{:S(2)}) async-start(bf16[32,40,128]{2,1,0:T(8,128)(2,1)} %shard_map.175), calls=%async_computation.1 | async-start | bytes 655360 | tf_op jit(solution)/shard_map/all_to_all | solution.py:406
  42.3 7.8 %copy-start.4 = (s32[8,32]{1,0:T(8,128)S(1)}, s32[8,32]{1,0:T(8,128)}, u32[]{:S(2)}) copy-start(s32[8,32]{1,0:T(8,128)} %param.23) | copy-start | bytes 3076
  42.3 8.9 %copy-start.3 = (bf16[2048,64]{0,1:T(8,128)(2,1)S(1)}, bf16[2048,64]{0,1:T(8,128)(2,1)}, u32[]{:S(2)}) copy-start(bf16[2048,64]{0,1:T(8,128)(2,1)} %param.18) | copy-start | bytes 786436
  43.3 22.7 %all-to-all-start.2 = ((bf16[32,80,128]{2,1,0:T(8,128)(2,1)}), bf16[32,80,128]{2,1,0:T(8,128)(2,1)S(1)}, u32[]{:S(2)}, u32[]{:S(2)}) async-start(bf16[32,80,128]{2,1,0:T(8,128)(2,1)} %shard_map.177), calls=%async_computation.2 | async-start | bytes 1310720 | tf_op jit(solution)/shard_map/all_to_all | solution.py:425
  51.2 23.8 %copy-start.6 = (bf16[2048]{0:T(1024)(128)(2,1)S(1)}, bf16[2048]{0:T(1024)(128)(2,1)}, u32[]{:S(2)}) copy-start(bf16[2048]{0:T(1024)(128)(2,1)} %param.24) | copy-start | bytes 12292
  51.3 23.8 %copy-start.7 = (s32[4,2]{0,1:T(2,128)S(1)}, s32[4,2]{0,1:T(2,128)}, u32[]{:S(2)}) copy-start(s32[4,2]{0,1:T(2,128)} %param.26) | copy-start | bytes 100
  51.3 23.9 %copy-start.8 = (s32[64]{0:T(128)S(1)}, s32[64]{0:T(128)}, u32[]{:S(2)}) copy-start(s32[64]{0:T(128)} %param.27) | copy-start | bytes 772
  67.4 35.0 %copy-start.2 = (bf16[2048,400]{0,1:T(8,128)(2,1)S(1)}, bf16[2048,400]{0,1:T(8,128)(2,1)}, u32[]{:S(2)}) copy-start(bf16[2048,400]{0,1:T(8,128)(2,1)} %param.25) | copy-start | bytes 4915204
  67.4 17.9 %all-to-all-start.3 = ((bf16[32,48,128]{2,1,0:T(8,128)(2,1)}), bf16[32,48,128]{2,1,0:T(8,128)(2,1)S(1)}, u32[]{:S(2)}, u32[]{:S(2)}) async-start(bf16[32,48,128]{2,1,0:T(8,128)(2,1)} %get-tuple-element.13), calls=%async_computation.3 | async-start | bytes 786432 | tf_op jit(solution)/shard_map/all_to_all | solution.py:454
  86.1 16.2 %all-to-all-start.4 = ((bf16[8,8,2048]{2,1,0:T(8,128)(2,1)}), bf16[8,8,2048]{2,1,0:T(8,128)(2,1)S(1)}, u32[]{:S(2)}, u32[]{:S(2)}) async-start(bf16[8,8,2048]{2,1,0:T(8,128)(2,1)} %get-tuple-element.16), calls=%async_computation.4 | async-start | bytes 524288 | tf_op jit(solution)/shard_map/all_to_all | solution.py:466
  103.7 19.8 %all-to-all-start.5 = ((f32[256,1,128]{2,1,0:T(1,128)}), f32[256,1,128]{2,1,0:T(1,128)S(1)}, u32[]{:S(2)}, u32[]{:S(2)}) async-start(f32[256,1,128]{2,1,0:T(1,128)} %bitcast.42), calls=%async_computation.5 | async-start | bytes 262144 | tf_op jit(solution)/shard_map/all_to_all | solution.py:478
